TPU v7x, 256 devices: a whole 4x4x8 slice. The times are simulated.
256 devices in a mesh: seq: 64 (over y, z_lo, x), tp: 4 (over z_hi, core).
Axes of the slice: x: 4, y: 4, z: 8 (z_hi: 2, z_lo: 4; z = z_hi * 4 + z_lo), core: 2. Of those that a mesh axis runs over, the one named last changes fastest.
Arguments:
- tokens: bfloat16 [32768, 5376], P(('seq', 'tp')), may hold values from -180 to 180
- in_gain: float32 [5376], replicated, may hold values from 0.5 to 1.5
- raw_queries: bfloat16 [32768, 2048], P('seq', 'tp'), may hold values from -6 to 6
- w_key: bfloat16 [5376, 1024], P(None, 'tp'), may hold values from -0.078125 to 0.078125
- w_value: bfloat16 [5376, 1024], P(None, 'tp'), may hold values from -0.078125 to 0.078125
- q_gain: float32 [128], replicated, may hold values from 0.5 to 1.5
- k_gain: float32 [128], replicated, may hold values from 0.5 to 1.5
- doc_lengths: int32 [32], replicated, may hold values from 1 to 4096, as said below
- out_grad: bfloat16 [32768, 2048], P('seq', 'tp'), may hold values from -60 to 60
Outputs:
- grad_x: bfloat16 [32768, 5376], P(('seq', 'tp'))
- grad_queries: bfloat16 [32768, 2048], P('seq', 'tp')
- grad_wk: float32 [5376, 1024], P('seq', 'tp')
- grad_wv: float32 [5376, 1024], P('seq', 'tp')
Inputs may be any that keep to these rules, and one draw needn't show every extreme that they name: `doc_lengths`: the 32 lengths sum to 32768; the last rollout is the longest, exactly 4096 tokens.
All inputs are finite; a program needn't handle non-finite values.
Results may differ from a plain program's by a relative error of at most 0.014.
Values may be sent and summed in bfloat16 or wider, within the bound.
A program may use at most 128 MiB of HBM per device.

v0:
```python
import jax
import jax.numpy as jnp
from jax import lax
from jax.sharding import PartitionSpec as P

WINDOW = 1024


EPSILON = 1e-06
QUERY_SCALE = 168.0 ** (-0.5)
ROPE_BASE = 10000.0


def from_behind(array, axis, by):
    size = lax.axis_size(axis)
    pairs = [(i, i + by) for i in range(size) if 0 <= i + by < size]
    return lax.ppermute(array, axis, pairs)


def doc_begin(doc_lengths, positions):
    endings = jnp.cumsum(doc_lengths, dtype=jnp.int32)
    starts = endings - doc_lengths
    inside = starts[None, :] <= positions[:, None]
    return jnp.max(jnp.where(inside, starts[None, :], jnp.zeros_like(starts)[None, :]), axis=1)


def input_norm(values, gain):
    return values * lax.rsqrt(jnp.mean(values * values, axis=1, keepdims=True) + EPSILON) * gain


def head_norm(values, gain):
    return values * lax.rsqrt(jnp.mean(values * values, axis=-1, keepdims=True) + EPSILON) * gain


def rotate(values, positions):
    half_size = values.shape[-1] // 2
    powers = jnp.arange(half_size, dtype=jnp.float32) * (2.0 / values.shape[-1])
    frequency = ROPE_BASE ** (-powers)
    angles = positions.astype(jnp.float32)[:, None] * frequency[None, :]
    cosine = jnp.cos(angles)[:, None, :]
    sine = jnp.sin(angles)[:, None, :]
    first = values[..., :half_size]
    second = values[..., half_size:]
    return jnp.concatenate(
        [first * cosine - second * sine, second * cosine + first * sine], axis=-1
    )


def contract_last(left, right):
    return lax.dot_general(
        left, right, (((1,), (1,)), ((), ())), preferred_element_type=jnp.float32
    )


def contract_first(left, right):
    return lax.dot_general(
        left, right, (((0,), (0,)), ((), ())), preferred_element_type=jnp.float32
    )


def attend(queries, key_rows, value_rows, grads, lowest, positions, key_positions):
    scores = jnp.einsum("qkgd,skd->kgqs", queries, key_rows, preferred_element_type=jnp.float32)
    allowed = (key_positions[None, :] >= lowest[:, None]) & (
        key_positions[None, :] <= positions[:, None]
    )
    exps = jnp.where(allowed[None, None], jnp.exp(scores), jnp.zeros_like(scores))
    totals = jnp.sum(exps, axis=-1, keepdims=True)
    probs = exps / totals
    rounded = probs.astype(jnp.bfloat16)
    outputs = jnp.einsum("kgqs,skd->qkgd", rounded, value_rows, preferred_element_type=jnp.float32)
    deltas = jnp.sum(grads.astype(jnp.float32) * outputs, axis=-1)
    along = jnp.einsum("qkgd,skd->kgqs", grads, value_rows, preferred_element_type=jnp.float32)
    slopes = (probs * (along - jnp.transpose(deltas, (1, 2, 0))[..., None])).astype(jnp.bfloat16)
    query_grad = jnp.einsum("kgqs,skd->qkgd", slopes, key_rows, preferred_element_type=jnp.float32)
    key_grad = jnp.einsum("kgqs,qkgd->skd", slopes, queries, preferred_element_type=jnp.float32)
    value_grad = jnp.einsum("kgqs,qkgd->skd", rounded, grads, preferred_element_type=jnp.float32)
    return (query_grad, key_grad, value_grad)


def shards(tokens, in_gain, raw_queries, w_key, w_value, q_gain, k_gain, doc_lengths, out_grad):
    tp_count = lax.axis_size("tp")
    head_size = q_gain.shape[0]
    kv_heads = w_key.shape[1] // head_size
    group_size = raw_queries.shape[1] // w_key.shape[1]
    shard_rows = tokens.shape[0] * tp_count
    reach_count = (WINDOW - 2) // shard_rows + 1
    x_float = tokens.astype(jnp.float32)
    normed_rows = input_norm(x_float, in_gain).astype(jnp.bfloat16)
    gathered = lax.all_gather(normed_rows, "tp", axis=0, tiled=True)
    first_row = lax.axis_index("seq") * shard_rows
    positions = first_row + jnp.arange(shard_rows, dtype=jnp.int32)
    begins = doc_begin(doc_lengths, positions)
    offsets = positions - begins
    lowest = jnp.maximum(begins, positions - (WINDOW - 1))
    queries = raw_queries.astype(jnp.float32).reshape(shard_rows, -1, head_size)
    keys_raw = jnp.dot(gathered, w_key, preferred_element_type=jnp.float32).reshape(
        shard_rows, -1, head_size
    )
    values_raw = jnp.dot(gathered, w_value, preferred_element_type=jnp.float32).reshape(
        shard_rows, -1, head_size
    )

    def query_map(values):
        return rotate(head_norm(values, q_gain), offsets) * QUERY_SCALE

    def key_map(values):
        return rotate(head_norm(values, k_gain), offsets)

    query_rot, query_back = jax.vjp(query_map, queries)
    key_rot, key_back = jax.vjp(key_map, keys_raw)
    query_rows = query_rot.astype(jnp.bfloat16).reshape(shard_rows, kv_heads, group_size, head_size)
    key_rows = key_rot.astype(jnp.bfloat16)
    value_rows = values_raw.astype(jnp.bfloat16)
    grad_rows = out_grad.reshape(shard_rows, kv_heads, group_size, head_size)
    rim_keys = []
    rim_values = []
    for distance in range(reach_count, 0, -1):
        far_keys, far_values = from_behind((key_rows, value_rows), "seq", distance)
        rim_keys.append(far_keys)
        rim_values.append(far_values)
    key_window = jnp.concatenate(rim_keys + [key_rows], axis=0)
    value_window = jnp.concatenate(rim_values + [value_rows], axis=0)
    key_positions = (
        first_row
        - reach_count * shard_rows
        + jnp.arange((reach_count + 1) * shard_rows, dtype=jnp.int32)
    )
    query_grad, key_grad_all, value_grad_all = attend(
        query_rows, key_window, value_window, grad_rows, lowest, positions, key_positions
    )
    own_start = reach_count * shard_rows
    key_grad = key_grad_all[own_start:]
    value_grad = value_grad_all[own_start:]
    for distance in range(1, reach_count + 1):
        lower_row = (reach_count - distance) * shard_rows
        back_keys, back_values = (
            from_behind(
                key_grad_all[lower_row : lower_row + shard_rows].astype(jnp.bfloat16),
                "seq",
                -distance,
            ).astype(jnp.float32),
            from_behind(
                value_grad_all[lower_row : lower_row + shard_rows].astype(jnp.bfloat16),
                "seq",
                -distance,
            ).astype(jnp.float32),
        )
        key_grad = key_grad + back_keys
        value_grad = value_grad + back_values
    query_grad = query_grad.reshape(shard_rows, kv_heads * group_size, head_size)
    grad_queries = query_back(query_grad)[0].reshape(shard_rows, -1).astype(jnp.bfloat16)
    grad_k = key_back(key_grad)[0].reshape(shard_rows, -1).astype(jnp.bfloat16)
    grad_v = value_grad.reshape(shard_rows, -1).astype(jnp.bfloat16)
    partial_sum = contract_last(grad_k, w_key) + contract_last(grad_v, w_value)
    normed_grad = lax.psum_scatter(
        partial_sum.astype(jnp.bfloat16), "tp", scatter_dimension=0, tiled=True
    ).astype(jnp.float32)

    def norm_map(values):
        return input_norm(values, in_gain)

    unused_rows, norm_back = jax.vjp(norm_map, x_float)
    grad_x = norm_back(normed_grad)[0].astype(jnp.bfloat16)
    grads_joined = jnp.concatenate([grad_k, grad_v], axis=1)
    weight_term = contract_first(gathered, grads_joined)
    summed = lax.psum_scatter(weight_term, "seq", scatter_dimension=0, tiled=True)
    kv_cols = w_key.shape[1]
    grad_wk = summed[:, :kv_cols]
    grad_wv = summed[:, kv_cols:]
    return (grad_x, grad_queries, grad_wk, grad_wv)


def solution(mesh):
    placed = (
        P(("seq", "tp"), None),
        P(),
        P("seq", "tp"),
        P(None, "tp"),
        P(None, "tp"),
        P(),
        P(),
        P(),
        P("seq", "tp"),
    )
    return jax.shard_map(
        shards,
        mesh=mesh,
        in_specs=placed,
        out_specs=(P(("seq", "tp"), None), P("seq", "tp"), P("seq", "tp"), P("seq", "tp")),
        check_vma=False,
    )
```

profile of v0, /device:TPU:2, one launch (start us, length us, event | category | flops | bytes accessed | tf_op | source)
XLA Modules:
  0.0 1047.0 jit_solution(17603129184063774327)
XLA Ops:
  7.2 1.8 fusion.6
  10.1 2.8 fusion.8
  13.3 1.3 reshape.249
  14.6 1.9 multiply_reduce_fusion.1
  17.9 1.8 multiply_multiply_fusion
  19.7 1.1 multiply_subtract_fusion
  24.0 2.7 fusion.13
  26.7 1.6 compare_and_fusion
  28.3 68.9 %all-gather.2.cloned.1.call-done = bf16[512,5376]{1,0:T(8,128)(2,1)} async-done(((bf16[128,5376]{1,0:T(8,128)(2,1)}), bf16[512,5376]{1,0:T(8,128)(2,1)}) %all-gather.2.cloned.1.call-update) | async-done | bytes 5505040 | tf_op jit(solution)/shard_map/all_gather | solution.py:89
  97.2 5.0 multiply_reduce_fusion.3
  102.2 1.2 copy.134
  104.5 1.2 subtract_convert_fusion
  107.2 4.7 collective-permute-start
  111.9 1.9 collective-permute-start.1
  113.8 4.9 convolution_convert_fusion
  118.7 1.8 copy.135
  120.5 4.5 collective-permute-start.2
  125.1 2.1 collective-permute-start.3
  127.2 5.1 fusion.3
  132.3 2.1 fusion.4
  134.4 2.9 collective-permute-done.3
  137.3 1.1 fusion.11
  138.4 6.9 fusion.1
  145.3 4.6 fusion.35
  150.0 1.9 collective-permute-start.4
  151.9 1.3 collective-permute-start.5
  153.2 3.3 fusion.36
  157.4 1.9 collective-permute-start.6
  159.3 1.5 collective-permute-start.7
  160.9 7.2 collective-permute-done.5
  168.9 1.2 fusion.14
  170.0 1.1 copy.147
  171.1 1.7 fusion.37
  173.7 4.3 collective-permute-done.7
  178.0 1.3 fusion.16
  179.3 4.0 add_convert_fusion
  183.4 8.8 fusion.18
  194.3 4.7 convolution_multiply_fusion
  200.0 2.5 copy.172
  202.6 2.4 copy.173
  205.0 2.2 multiply_add_fusion.1
  208.5 1.2 multiply_reduce_fusion
  210.0 3.7 fusion.12
  214.6 69.0 %reduce-scatter.2.cloned.1.call-done = bf16[128,5376]{1,0:T(8,128)(2,1)} async-done(((bf16[512,5376]{1,0:T(8,128)(2,1)}), bf16[128,5376]{1,0:T(8,128)(2,1)}) %reduce-scatter.2.cloned.1.call-update) | async-done | bytes 1376272 | tf_op jit(solution)/shard_map/reduce_scatter | solution.py:155
  283.6 2.4 fusion.9
  286.2 1.8 fusion.5
  288.0 750.7 %all-reduce.7.cloned.1.call-done = f32[5376,512]{1,0:T(8,128)} async-done(((f32[5376,512]{1,0:T(8,128)}), f32[5376,512]{1,0:T(8,128)}) %all-reduce.7.cloned.1.call-update) | async-done | bytes 11010064
  1038.8 1.7 fusion.31
  (108 shorter events, 16.1 us)
Async XLA Ops:
  7.2 90.0 %copy-start = (bf16[5376,256]{1,0:T(8,128)(2,1)S(1)}, bf16[5376,256]{1,0:T(8,128)(2,1)}, u32[]{:S(2)}) copy-start(bf16[5376,256]{1,0:T(8,128)(2,1)} %param.12) | copy-start | bytes 8257540
  7.2 5.8 copy-start.30
  7.2 6.1 copy-start.20
  7.2 90.0 %all-gather.2.cloned.1.call-start = ((), (), s32[]{:S(2)}) async-start(), calls=%async_computation.1 | async-start | bytes 6881280 | tf_op jit(solution)/shard_map/all_gather | solution.py:89
  9.1 0.5 copy-start.28
  9.6 0.5 copy-start.26
  12.9 270.7 %reduce-scatter.2.cloned.1.call-start = ((), (), s32[]{:S(2)}) async-start(), calls=%async_computation.2 | async-start | bytes 6881280 | tf_op jit(solution)/shard_map/reduce_scatter | solution.py:155
  16.7 4.1 copy-start.12
  17.9 3.0 copy-start.5
  20.9 2.1 copy-start.21
  103.4 10.4 copy-start.10
  105.7 0.7 copy-start.16
  105.7 1.6 copy-start.18
  107.2 19.9 %collective-permute-start = (bf16[512,2,128]{2,0,1:T(8,128)(2,1)}, bf16[512,2,128]{2,0,1:T(8,128)(2,1)}, u32[]{:S(2)}, u32[]{:S(2)}) collective-permute-start(bf16[512,2,128]{2,0,1:T(8,128)(2,1)} %pad_maximum_fusion), channel_id=1, source_target_pairs={{0,8},{4,12},{8,16},{12,20},{16,24},{20,28},{24,32},{28,36},{32,40... | collective-permute-start | bytes 786440 | tf_op jit(solution)/shard_map/ppermute | solution.py:17
  111.9 15.3 %collective-permute-start.1 = (bf16[512,2,128]{2,0,1:T(8,128)(2,1)}, bf16[512,2,128]{2,0,1:T(8,128)(2,1)}, u32[]{:S(2)}, u32[]{:S(2)}) collective-permute-start(bf16[512,2,128]{2,0,1:T(8,128)(2,1)} %pad_maximum_fusion), channel_id=1, source_target_pairs={{0,4},{4,8},{8,12},{12,16},{16,20},{20,24},{24,28},{28,32},{32,36}... | collective-permute-start | bytes 786440 | tf_op jit(solution)/shard_map/ppermute | solution.py:17
  120.5 11.7 %copy-start.9 = (pred[512,1536]{0,1:T(8,128)(4,1)S(1)}, pred[512,1536]{0,1:T(8,128)(4,1)}, u32[]{:S(2)}) copy-start(pred[512,1536]{0,1:T(8,128)(4,1)} %compare_and_fusion) | copy-start | bytes 2359300
  120.5 13.9 %collective-permute-start.2 = (bf16[512,2,128]{2,0,1:T(8,128)(2,1)}, bf16[512,2,128]{2,0,1:T(8,128)(2,1)S(1)}, u32[]{:S(2)}, u32[]{:S(2)}) collective-permute-start(bf16[512,2,128]{2,0,1:T(8,128)(2,1)} %copy.135), channel_id=1, source_target_pairs={{0,8},{4,12},{8,16},{12,20},{16,24},{20,28},{24,32},{28,36},{32,40... | collective-permute-start | bytes 786440 | tf_op jit(solution)/shard_map/ppermute | solution.py:17
  125.1 12.3 %collective-permute-start.3 = (bf16[512,2,128]{2,0,1:T(8,128)(2,1)}, bf16[512,2,128]{2,0,1:T(8,128)(2,1)S(1)}, u32[]{:S(2)}, u32[]{:S(2)}) collective-permute-start(bf16[512,2,128]{2,0,1:T(8,128)(2,1)} %copy.135), channel_id=1, source_target_pairs={{0,4},{4,8},{8,12},{12,16},{16,20},{20,24},{24,28},{28,32},{32,36}... | collective-permute-start | bytes 786440 | tf_op jit(solution)/shard_map/ppermute | solution.py:17
  132.3 5.1 copy-start.15
  132.3 5.1 copy-start.22
  138.4 6.9 copy-start.14
  150.0 10.8 %collective-permute-start.4 = (bf16[512,2,128]{2,0,1:T(8,128)(2,1)S(1)}, bf16[512,2,128]{2,0,1:T(8,128)(2,1)S(1)}, u32[]{:S(2)}, u32[]{:S(2)}) collective-permute-start(bf16[512,2,128]{2,0,1:T(8,128)(2,1)S(1)} %get-tuple-element.18), channel_id=1, source_target_pairs={{4,0},{8,4},{12,8},{16,12},{20,16},{24,20},{28,24},{32,28},{36,32}... | collective-permute-start | bytes 786440 | tf_op jit(solution)/shard_map/ppermute | solution.py:17
  151.9 16.2 %collective-permute-start.5 = (bf16[512,2,128]{2,0,1:T(8,128)(2,1)S(1)}, bf16[512,2,128]{2,0,1:T(8,128)(2,1)S(1)}, u32[]{:S(2)}, u32[]{:S(2)}) collective-permute-start(bf16[512,2,128]{2,0,1:T(8,128)(2,1)S(1)} %get-tuple-element.19), channel_id=1, source_target_pairs={{8,0},{12,4},{16,8},{20,12},{24,16},{28,20},{32,24},{36,28},{40,32... | collective-permute-start | bytes 786440 | tf_op jit(solution)/shard_map/ppermute | solution.py:17
  156.6 11.6 %copy-start.6 = (f32[512,64]{1,0:T(8,128)S(1)}, f32[512,64]{1,0:T(8,128)}, u32[]{:S(2)}) copy-start(f32[512,64]{1,0:T(8,128)} %copy-done.5) | copy-start | bytes 393220
  156.6 11.9 %copy-start.25 = (f32[128]{0:T(128)S(1)}, f32[128]{0:T(128)}, u32[]{:S(2)}) copy-start(f32[128]{0:T(128)} %param.15) | copy-start | bytes 1540
  157.4 16.3 %collective-permute-start.6 = (bf16[512,2,128]{0,2,1:T(8,128)(2,1)}, bf16[512,2,128]{0,2,1:T(8,128)(2,1)}, u32[]{:S(2)}, u32[]{:S(2)}) collective-permute-start(bf16[512,2,128]{0,2,1:T(8,128)(2,1)} %get-tuple-element.16), channel_id=1, source_target_pairs={{4,0},{8,4},{12,8},{16,12},{20,16},{24,20},{28,24},{32,28},{36,32}... | collective-permute-start | bytes 786440 | tf_op jit(solution)/shard_map/ppermute | solution.py:17
  159.3 18.7 %collective-permute-start.7 = (bf16[512,2,128]{0,2,1:T(8,128)(2,1)}, bf16[512,2,128]{0,2,1:T(8,128)(2,1)}, u32[]{:S(2)}, u32[]{:S(2)}) collective-permute-start(bf16[512,2,128]{0,2,1:T(8,128)(2,1)} %get-tuple-element.17), channel_id=1, source_target_pairs={{8,0},{12,4},{16,8},{20,12},{24,16},{28,20},{32,24},{36,28},{40,32... | collective-permute-start | bytes 786440 | tf_op jit(solution)/shard_map/ppermute | solution.py:17
  171.1 8.2 copy-start.11
  183.4 855.4 %all-reduce.7.cloned.1.call-start = ((), (), s32[]{:S(2)}) async-start(), calls=%async_computation.3 | async-start | bytes 22020096
  192.2 0.7 copy-start.31
  192.2 2.0 copy-start.17
  192.2 2.0 copy-start.19
  198.9 6.0 copy-start.7
  204.9 3.6 copy-start.1
  205.0 3.6 copy-start.24
  207.2 1.0 copy-start.3
  207.2 1.3 copy-start.4
  207.2 2.8 copy-start.13
  209.8 73.8 %copy-start.23 = (f32[5376]{0:T(1024)S(1)}, f32[5376]{0:T(1024)}, u32[]{:S(2)}) copy-start(f32[5376]{0:T(1024)} %param.10) | copy-start | bytes 64516
  213.7 72.4 %copy-start.29 = (f32[128]{0:T(128)S(1)}, f32[128]{0:T(128)}, u32[]{:S(2)}) copy-start(f32[128]{0:T(128)} %copy-done.28) | copy-start | bytes 1540
  213.7 72.4 %copy-start.27 = (f32[128]{0:T(128)S(1)}, f32[128]{0:T(128)}, u32[]{:S(2)}) copy-start(f32[128]{0:T(128)} %copy-done.26) | copy-start | bytes 1540
  283.6 2.5 copy-start.2
  283.6 2.6 copy-start.8
Sparse Core Ops, SparseCore 0:
  13.1 84.0 all-gather.1
  183.5 100.0 reduce-scatter.1
  286.3 752.4 all-reduce.6
where the time goes:
time: 1050 us
  waiting for transfers between devices  904 us (86%)
  matrix products  50 us (5%)
  other arithmetic  34.7 us (3%)
  local copies, waits for them, and re-layouts  23.1 us (2%)
  starting transfers between devices  20 us (2%)
  between operations  15.1 us (1%)
    unnamed x4, waiting for transfers between devices  751 us
    reduce_scatter x1, waiting for transfers between devices, shards(): lax.psum_scatter(partial_sum.astype(jnp.bfloat16), 'tp', scatter_dimensio...  69 us
    all_gather x1, waiting for transfers between devices, shards(): gathered = lax.all_gather(normed_rows, 'tp', axis=0, tiled=True)  68.9 us
  transfers between devices with their start and end apart: 11, of which 7 were waited for; matrix products, arithmetic and copies ran while one was open for 7% of the time, Pallas kernels for 0%

commit v1 on v0

--- a/solution.py
+++ b/solution.py
@@ -1,6 +1,8 @@
 import jax
 import jax.numpy as jnp
 from jax import lax
+from jax.experimental import pallas as pl
+from jax.experimental.pallas import tpu as pltpu
 from jax.sharding import PartitionSpec as P
 
 WINDOW = 1024
@@ -75,6 +77,239 @@
     key_grad = jnp.einsum("kgqs,qkgd->skd", slopes, queries, preferred_element_type=jnp.float32)
     value_grad = jnp.einsum("kgqs,qkgd->skd", rounded, grads, preferred_element_type=jnp.float32)
     return (query_grad, key_grad, value_grad)
+
+
+MESH_IDS = pl.DeviceIdType.MESH
+
+
+def ring_sum(piece, size, split, pos, up, down, bufs, sems, finish):
+    half_up, half_down, mixed_up, mixed_down, full_up, full_down = bufs
+    send_sem, recv_sem = sems
+    far = lax.rem(pos + 2, 4)
+    after = lax.rem(pos + 1, 4)
+    before = lax.rem(pos + 3, 4)
+    low = pl.ds(0, split)
+    high = pl.ds(split, size - split)
+
+    def copy(index, source, target, device):
+        return pltpu.make_async_remote_copy(
+            src_ref=source,
+            dst_ref=target,
+            send_sem=send_sem.at[index],
+            recv_sem=recv_sem.at[index],
+            device_id=device,
+            device_id_type=MESH_IDS,
+        )
+
+    first = [
+        copy(0, piece(far).at[low], half_up, up),
+        copy(1, piece(far).at[high], half_down, down),
+        copy(2, piece(after).at[high], full_up.at[high], up),
+        copy(3, piece(before).at[low], full_down.at[low], down),
+    ]
+    for one in first:
+        one.start()
+
+    def second():
+        first[0].wait_recv()
+        mixed_up[...] = (
+            piece(after)[low, :].astype(jnp.float32) + half_up[...].astype(jnp.float32)
+        ).astype(jnp.bfloat16)
+        last_up = copy(4, mixed_up, full_up.at[low], up)
+        last_up.start()
+        first[1].wait_recv()
+        mixed_down[...] = (
+            piece(before)[high, :].astype(jnp.float32) + half_down[...].astype(jnp.float32)
+        ).astype(jnp.bfloat16)
+        last_down = copy(5, mixed_down, full_down.at[high], down)
+        last_down.start()
+
+        def third():
+            first[2].wait_recv()
+            first[3].wait_recv()
+            last_up.wait_recv()
+            last_down.wait_recv()
+            finish(
+                lambda rows: piece(pos)[rows, :].astype(jnp.float32)
+                + full_up[rows, :].astype(jnp.float32)
+                + full_down[rows, :].astype(jnp.float32)
+            )
+
+            def drain():
+                for one in first + [last_up, last_down]:
+                    one.wait_send()
+
+            return drain
+
+        return third
+
+    return second
+
+
+def weight_sum_kernel(
+    key_ref, value_ref, key_out, value_out,
+    key_send, order, value_total, key_next, value_next, last_send, last_recv,
+    *rest,
+):
+    bufs_a, bufs_b, bufs_c, bufs_d = rest[0:6], rest[6:12], rest[12:18], rest[18:24]
+    sems = rest[24:]
+    rows = key_out.shape[0]
+    cols = key_out.shape[1]
+    big, mid = 16 * rows, 4 * rows
+    split_big = big // 2
+    split_mid = mid // 2 + mid // 2 % 16
+    place = lax.axis_index("seq")
+    member = lax.axis_index("tp")
+    x = lax.rem(place, 4)
+    z = lax.rem(place // 4, 4)
+    y = place // 16
+
+    def device(ys, zs, xs):
+        return ((ys * 4 + zs) * 4 + xs, member)
+
+    x_up, x_down = device(y, z, lax.rem(x + 1, 4)), device(y, z, lax.rem(x + 3, 4))
+    y_up, y_down = device(lax.rem(y + 1, 4), z, x), device(lax.rem(y + 3, 4), z, x)
+    z_others = [device(y, lax.rem(z + d, 4), x) for d in (1, 2, 3)]
+    barrier = pltpu.get_barrier_semaphore()
+    for other in [x_up, x_down, y_up, y_down] + z_others:
+        pl.semaphore_signal(barrier, inc=1, device_id=other, device_id_type=MESH_IDS)
+
+    pl.semaphore_wait(barrier, 7)
+
+    def finish_b1(total):
+        for part in range(4):
+            at = pl.ds(part * mid, mid)
+            value_total[at, :] = total(at)
+        for xs in range(4):
+            for zs in range(4):
+                order[zs * rows : zs * rows + rows, :] = value_total[
+                    zs * mid + xs * rows : zs * mid + xs * rows + rows, :
+                ]
+            value_next[xs] = order[...].astype(jnp.bfloat16)
+
+    second_b = ring_sum(
+        lambda t: value_ref.at[pl.ds(pl.multiple_of(t * big, 16), big)],
+        big, split_big, y, y_up, y_down, bufs_b, sems[2:4], finish_b1,
+    )
+
+    for ys in range(4):
+        for xs in range(4):
+            for zs in range(4):
+                begin = ((ys * 4 + zs) * 4 + xs) * rows
+                order[zs * rows : zs * rows + rows, :] = key_ref[begin : begin + rows, :]
+            key_send[xs, ys * mid : ys * mid + mid, :] = order[...].astype(jnp.bfloat16)
+
+    def finish_a1(total):
+        for part in range(4):
+            at = pl.ds(part * mid, mid)
+            key_next[part] = total(at).astype(jnp.bfloat16)
+
+    second_a = ring_sum(
+        lambda t: key_send.at[t],
+        big, split_big, x, x_up, x_down, bufs_a, sems[0:2], finish_a1,
+    )
+    third_b = second_b()
+    third_a = second_a()
+    drain_b = third_b()
+
+    def finish_last(at):
+        def finish(total):
+            order[...] = total(pl.ds(0, mid))
+            for zs in range(4):
+                last_send[zs, 0:rows, at : at + cols] = order[
+                    zs * rows : zs * rows + rows, :
+                ].astype(jnp.bfloat16)
+                last_send[zs, rows:, at : at + cols] = jnp.zeros(
+                    (last_send.shape[1] - rows, cols), jnp.bfloat16
+                )
+
+        return finish
+
+    second_d = ring_sum(
+        lambda t: value_next.at[t],
+        mid, split_mid, x, x_up, x_down, bufs_d, sems[6:8], finish_last(cols),
+    )
+    drain_a = third_a()
+    second_c = ring_sum(
+        lambda t: key_next.at[t],
+        mid, split_mid, y, y_up, y_down, bufs_c, sems[4:6], finish_last(0),
+    )
+    third_d = second_d()
+    third_c = second_c()
+    drain_d = third_d()
+    drain_c = third_c()
+    copies = []
+    for d in (1, 2, 3):
+        one = pltpu.make_async_remote_copy(
+            src_ref=last_send.at[lax.rem(z + d, 4)],
+            dst_ref=last_recv.at[d - 1],
+            send_sem=sems[8].at[d - 1],
+            recv_sem=sems[9].at[d - 1],
+            device_id=z_others[d - 1],
+            device_id_type=MESH_IDS,
+        )
+        one.start()
+        copies.append(one)
+    for one in copies:
+        one.wait_recv()
+    total = last_send[z, 0:rows, :].astype(jnp.float32)
+    for d in range(3):
+        total = total + last_recv[d, 0:rows, :].astype(jnp.float32)
+    key_out[...] = total[:, 0:cols]
+    value_out[...] = total[:, cols:]
+    for one in copies:
+        one.wait_send()
+    for drain in (drain_a, drain_b, drain_c, drain_d):
+        drain()
+
+
+def weight_sum(key_term, value_term):
+    depth, cols = key_term.shape
+    rows = depth // 64
+    big, mid = 16 * rows, 4 * rows
+    split_big = big // 2
+    split_mid = mid // 2 + mid // 2 % 16
+    padded = (rows + 15) // 16 * 16
+    bf = jnp.bfloat16
+
+    def bufs(size, split):
+        return [
+            pltpu.VMEM((split, cols), bf),
+            pltpu.VMEM((size - split, cols), bf),
+            pltpu.VMEM((split, cols), bf),
+            pltpu.VMEM((size - split, cols), bf),
+            pltpu.VMEM((size, cols), bf),
+            pltpu.VMEM((size, cols), bf),
+        ]
+
+    return pl.pallas_call(
+        weight_sum_kernel,
+        out_shape=[jax.ShapeDtypeStruct((rows, cols), jnp.float32)] * 2,
+        in_specs=[pl.BlockSpec(memory_space=pltpu.VMEM)] * 2,
+        out_specs=[pl.BlockSpec(memory_space=pltpu.VMEM)] * 2,
+        scratch_shapes=[
+            pltpu.VMEM((4, big, cols), bf),
+            pltpu.VMEM((mid, cols), jnp.float32),
+            pltpu.VMEM((big, cols), jnp.float32),
+            pltpu.VMEM((4, mid, cols), bf),
+            pltpu.VMEM((4, mid, cols), bf),
+            pltpu.VMEM((4, padded, 2 * cols), bf),
+            pltpu.VMEM((3, padded, 2 * cols), bf),
+        ]
+        + bufs(big, split_big)
+        + bufs(big, split_big)
+        + bufs(mid, split_mid)
+        + bufs(mid, split_mid)
+        + [pltpu.SemaphoreType.DMA((6,))] * 8
+        + [pltpu.SemaphoreType.DMA((3,))] * 2,
+        compiler_params=pltpu.CompilerParams(
+            collective_id=1, has_side_effects=True, vmem_limit_bytes=40 * 1024 * 1024
+        ),
+        cost_estimate=pl.CostEstimate(
+            flops=100_000_000, bytes_accessed=150_000_000, transcendentals=0
+        ),
+        name="weight_sum",
+    )(key_term, value_term)
 
 
 def shards(tokens, in_gain, raw_queries, w_key, w_value, q_gain, k_gain, doc_lengths, out_grad):
@@ -161,12 +396,9 @@
 
     unused_rows, norm_back = jax.vjp(norm_map, x_float)
     grad_x = norm_back(normed_grad)[0].astype(jnp.bfloat16)
-    grads_joined = jnp.concatenate([grad_k, grad_v], axis=1)
-    weight_term = contract_first(gathered, grads_joined)
-    summed = lax.psum_scatter(weight_term, "seq", scatter_dimension=0, tiled=True)
-    kv_cols = w_key.shape[1]
-    grad_wk = summed[:, :kv_cols]
-    grad_wv = summed[:, kv_cols:]
+    key_term = contract_first(gathered, grad_k)
+    value_term = contract_first(gathered, grad_v).astype(jnp.bfloat16)
+    grad_wk, grad_wv = weight_sum(key_term, value_term)
     return (grad_x, grad_queries, grad_wk, grad_wv)
 
 

time: 1050 us -> 306 us (0.29)
  the two profiles are of different devices: /device:TPU:2 before, /device:TPU:61 now
where the time goes in v1:
time: 306 us; the launch traced here: 303 us
  waiting for transfers between devices  76.7 us (25%)
  Pallas kernels  75.7 us (25%)
  matrix products  47.5 us (16%)
  other arithmetic  34.4 us (11%)
  starting transfers between devices  30.8 us (10%)
  local copies, waits for them, and re-layouts  23.3 us (8%)
  between operations  14.7 us (5%)
    pallas_call x1, Pallas kernels, weight_sum(): pl.pallas_call(weight_sum_kernel, out_shape=[jax.ShapeDtypeStruct((rows,...  75.7 us
    all_gather x1, waiting for transfers between devices, shards(): gathered = lax.all_gather(normed_rows, 'tp', axis=0, tiled=True)  69.8 us
    ppermute x8, starting transfers between devices, from_behind(): return lax.ppermute(array, axis, pairs)  30.7 us
    unnamed x74, local copies, waits for them, and re-layouts  13.8 us
    dot_general x1, matrix products, attend(): jnp.einsum('qkgd,skd->kgqs', grads, value_rows, preferred_element_type=jn...  6.88 us
    dot_general x2, matrix products, contract_first(): lax.dot_general(left, right, (((0,), (0,)), ((), ())), preferred_element_...  6.84 us
  transfers between devices with their start and end apart: 10, of which 4 were waited for; matrix products, arithmetic and copies ran while one was open for 21% of the time, Pallas kernels for 25%

profile of v1, /device:TPU:61, one launch (start us, length us, event | category | flops | bytes accessed | tf_op | source)
XLA Modules:
  0.0 303.1 jit_solution(9058684519746900774)
XLA Ops:
  7.2 1.8 fusion.6
  10.1 2.8 fusion.8
  13.3 2.1 copy.138
  15.3 1.3 reshape.249
  16.6 1.9 multiply_reduce_fusion.1
  19.9 1.8 multiply_multiply_fusion
  21.8 1.1 multiply_subtract_fusion
  23.1 1.1 fusion.13
  24.2 1.6 compare_and_fusion
  25.8 69.8 %all-gather.2.cloned.1.call-done = bf16[512,5376]{1,0:T(8,128)(2,1)} async-done(((bf16[128,5376]{1,0:T(8,128)(2,1)}), bf16[512,5376]{1,0:T(8,128)(2,1)}) %all-gather.2.cloned.1.call-update) | async-done | bytes 5505040 | tf_op jit(solution)/shard_map/all_gather | solution.py:324
  95.6 5.0 %multiply_reduce_fusion.3 = (f32[512,2]{0,1:T(2,128)S(1)}, f32[512,256]{0,1:T(8,128)}) fusion(bf16[512,5376]{1,0:T(8,128)(2,1)} %all-gather.2.cloned.1.call-done, bf16[5376,256]{1,0:T(8,128)(2,1)S(1)} %copy-done), kind=kOutput, calls=%fused_computation.57 | convolution fusion | flops 1409547264 | bytes 8785920 | tf_op jit(solution)/shard_map/dot_general | solution.py:331
  100.6 1.2 copy.134
  102.9 1.2 subtract_convert_fusion
  105.6 2.8 collective-permute-start.1
  108.4 2.2 collective-permute-start
  110.7 4.9 %convolution_convert_fusion.1 = bf16[512,256]{0,1:T(8,128)(2,1)} fusion(bf16[512,5376]{1,0:T(8,128)(2,1)} %all-gather.2.cloned.1.call-done, bf16[5376,256]{1,0:T(8,128)(2,1)S(1)} %copy-done.10), kind=kOutput, calls=%fused_computation.28 | convolution fusion | flops 1409417216 | bytes 8519680 | tf_op jit(solution)/shard_map/dot_general | solution.py:334
  115.6 1.8 copy.135
  117.4 3.8 %collective-permute-start.3 = (bf16[512,2,128]{2,0,1:T(8,128)(2,1)}, bf16[512,2,128]{2,0,1:T(8,128)(2,1)S(1)}, u32[]{:S(2)}, u32[]{:S(2)}) collective-permute-start(bf16[512,2,128]{2,0,1:T(8,128)(2,1)} %copy.135), channel_id=1, source_target_pairs={{0,4},{4,8},{8,12},{12,16},{16,20},{20,24},{24,28},{28,32},{32,36}... | collective-permute-start | bytes 786440 | tf_op jit(solution)/shard_map/ppermute | solution.py:19
  121.2 2.7 collective-permute-start.2
  124.0 5.1 %fusion.3 = (f32[2,2,512]{2,1,0:T(2,128)S(1)}, f32[2,1536,512,2]{2,1,3,0:T(8,128)S(1)}) fusion(pred[512,1536]{0,1:T(8,128)(4,1)} %compare_and_fusion, bf16[512,2,2,128]{3,0,2,1:T(8,128)(2,1)} %fusion.13, bf16[512,2,64]{2,0,1:T(8,128)(2,1)} %copy-done.20, bf16[512,2,64]{2,0,1:T(8,128)(2,1)} %copy-done.18, bf16[512,2,128]{2,0,1:T(8,128)(2,1)} %collective-permute-done.1, ...), kind=kOutput, calls=%fused_computation.5 | convolution fusion | flops 814741504 | bytes 14688256 | tf_op jit(solution)/shard_map/qkgd,skd->kgqs/dot_general | solution.py:64
  129.0 2.1 fusion.4
  131.2 2.5 collective-permute-done.2
  133.7 1.1 fusion.11
  134.8 6.9 %fusion.1 = bf16[2,2,512,1536]{2,3,1,0:T(8,128)(2,1)} fusion(bf16[512,2,2,128]{0,3,2,1:T(8,128)(2,1)S(1)} %bitcast.95, f32[2,2,512]{2,1,0:T(2,128)S(1)} %bitcast.105, f32[2,2,512]{2,1,0:T(2,128)S(1)} %get-tuple-element.28, f32[2,1536,512,2]{2,1,3,0:T(8,128)S(1)} %get-tuple-element.29, pred[512,1536]{0,1:T(8,128)(4,1)S(1)} %copy-done.9, ...), kind=kOutput, calls=%fused_computation.2 | convolution fusion | flops 823394304 | bytes 20987904 | tf_op jit(solution)/shard_map/qkgd,skd->kgqs/dot_general | solution.py:74
  141.7 4.6 %fusion.29 = (bf16[1536,2,128]{2,0,1:T(8,128)(2,1)S(1)}, f32[1536,2,128]{2,0,1:T(8,128)S(1)}) fusion(bf16[2,2,512,1536]{2,3,1,0:T(8,128)(2,1)} %fusion.1, bf16[512,2,2,128]{3,0,2,1:T(8,128)(2,1)S(1)} %copy-done.14), kind=kOutput, calls=%fused_computation.84 | convolution fusion | flops 805699584 | bytes 9175040 | tf_op jit(solution)/shard_map/kgqs,qkgd->skd/dot_general | solution.py:77
  146.4 6.0 %collective-permute-start.4 = (bf16[512,2,128]{2,0,1:T(8,128)(2,1)S(1)}, bf16[512,2,128]{2,0,1:T(8,128)(2,1)S(1)}, u32[]{:S(2)}, u32[]{:S(2)}) collective-permute-start(bf16[512,2,128]{2,0,1:T(8,128)(2,1)S(1)} %get-tuple-element.20), channel_id=1, source_target_pairs={{4,0},{8,4},{12,8},{16,12},{20,16},{24,20},{28,24},{32,28},{36,32}... | collective-permute-start | bytes 786440 | tf_op jit(solution)/shard_map/ppermute | solution.py:19
  152.4 1.9 collective-permute-start.5
  154.3 3.4 %fusion.30 = (bf16[1536,2,128]{0,2,1:T(8,128)(2,1)S(1)}, f32[1536,2,128]{0,2,1:T(8,128)}) fusion(bf16[2,2,512,1536]{2,3,1,0:T(8,128)(2,1)S(1)} %fusion.4, bf16[512,2,2,128]{0,3,2,1:T(8,128)(2,1)S(1)} %bitcast.96), kind=kOutput, calls=%fused_computation.85 | convolution fusion | flops 805699584 | bytes 9175040 | tf_op jit(solution)/shard_map/kgqs,qkgd->skd/dot_general | solution.py:78
  158.6 1.9 collective-permute-start.6
  160.5 9.3 %collective-permute-start.7 = (bf16[512,2,128]{0,2,1:T(8,128)(2,1)}, bf16[512,2,128]{0,2,1:T(8,128)(2,1)}, u32[]{:S(2)}, u32[]{:S(2)}) collective-permute-start(bf16[512,2,128]{0,2,1:T(8,128)(2,1)} %get-tuple-element.19), channel_id=1, source_target_pairs={{8,0},{12,4},{16,8},{20,12},{24,16},{28,20},{32,24},{36,28},{40,32... | collective-permute-start | bytes 786440 | tf_op jit(solution)/shard_map/ppermute | solution.py:19
  170.5 1.2 fusion.14
  171.7 1.1 copy.147
  172.8 1.7 fusion.31
  175.5 1.3 fusion.16
  177.5 4.0 %add_convert_fusion = bf16[512,5376]{1,0:T(8,128)(2,1)} fusion(f32[512,5376]{1,0:T(8,128)S(1)} %fusion.31, bf16[512,256]{0,1:T(8,128)(2,1)S(1)} %bitcast.98, bf16[5376,256]{1,0:T(8,128)(2,1)S(1)} %copy-done.11), kind=kOutput, calls=%fused_computation.6 | convolution fusion | flops 1414791168 | bytes 19529728 | tf_op jit(solution)/shard_map/dot_general | solution.py:52
  182.4 4.1 %convolution_multiply_fusion = f32[2,128,2,512]{3,1,2,0:T(8,128)S(1)} fusion(bf16[2,2,512,1536]{2,3,1,0:T(8,128)(2,1)} %fusion.1, bf16[512,2,64]{2,0,1:T(8,128)(2,1)} %copy-done.20, bf16[512,2,64]{2,0,1:T(8,128)(2,1)S(1)} %copy-done.19, bf16[512,2,128]{2,0,1:T(8,128)(2,1)} %collective-permute-done.1, bf16[512,2,128]{2,0,1:T(8,128)(2,1)} %collective-permute-done), kind=kOutput, calls=%fused_computation.24 | convolution fusion | flops 808714240 | bytes 8126464 | tf_op jit(solution)/shard_map/kgqs,skd->qkgd/dot_general | solution.py:76
  187.7 2.4 copy.172
  190.0 2.4 copy.173
  192.4 2.2 multiply_add_fusion.1
  196.0 1.2 multiply_reduce_fusion
  197.9 1.6 copy.154
  199.5 4.3 %fusion.12 = bf16[512,4,128]{2,1,0:T(4,128)(2,1)S(1)} fusion(f32[512,4,128]{2,1,0:T(4,128)} %reshape.249, f32[512,4]{1,0:T(8,128)} %copy.154, f32[512,4]{1,0:T(8,128)S(1)} %copy-done.13, f32[128]{0:T(128)} %param.14, f32[512,4,64]{2,1,0:T(4,128)} %copy-done.4, f32[512,4,64]{2,1,0:T(4,128)} %copy-done.3), kind=kLoop, calls=%fused_computation.29 | loop fusion | flops 1835008 | bytes 2638336 | tf_op jit(solution)/shard_map/convert_element_type | solution.py:386
  204.7 5.2 %convolution_convert_fusion.value_ref = bf16[5376,256]{1,0:T(8,128)(2,1)S(1)} fusion(bf16[512,5376]{1,0:T(8,128)(2,1)} %all-gather.2.cloned.1.call-done, bf16[512,256]{0,1:T(8,128)(2,1)S(1)} %bitcast.99), kind=kOutput, calls=%fused_computation.7 | convolution fusion | flops 1410662400 | bytes 8519680 | tf_op jit(solution)/shard_map/dot_general | solution.py:58
  209.9 1.6 fusion.32.key_ref
  211.6 75.7 %weight_sum.1 = (f32[84,256]{1,0:T(8,128)S(1)}, f32[84,256]{1,0:T(8,128)S(1)}) custom-call(f32[5376,256]{1,0:T(8,128)S(1)} %fusion.32.key_ref, bf16[5376,256]{1,0:T(8,128)(2,1)S(1)} %convolution_convert_fusion.value_ref), custom_call_target="tpu_custom_call" | custom-call | flops 100000000 | bytes 150000000 | tf_op jit(solution)/shard_map/weight_sum/pallas_call | solution.py:285
  287.3 3.4 %reduce-scatter.2.cloned.1.call-done = bf16[128,5376]{1,0:T(8,128)(2,1)} async-done(((bf16[512,5376]{1,0:T(8,128)(2,1)}), bf16[128,5376]{1,0:T(8,128)(2,1)}) %reduce-scatter.2.cloned.1.call-update) | async-done | bytes 1376272 | tf_op jit(solution)/shard_map/reduce_scatter | solution.py:390
  290.6 2.4 fusion.9
  293.2 1.8 fusion.5
  (112 shorter events, 15.1 us)
Async XLA Ops:
  7.2 88.4 %copy-start = (bf16[5376,256]{1,0:T(8,128)(2,1)S(1)}, bf16[5376,256]{1,0:T(8,128)(2,1)}, u32[]{:S(2)}) copy-start(bf16[5376,256]{1,0:T(8,128)(2,1)} %param.12) | copy-start | bytes 8257540
  7.2 5.8 %copy-start.31 = (s32[32]{0:T(128)S(1)}, s32[32]{0:T(128)}, u32[]{:S(2)}) copy-start(s32[32]{0:T(128)} %param.16) | copy-start | bytes 388
  7.2 88.4 %all-gather.2.cloned.1.call-start = ((), (), s32[]{:S(2)}) async-start(), calls=%async_computation.1 | async-start | bytes 6881280 | tf_op jit(solution)/shard_map/all_gather | solution.py:324
  9.1 0.5 copy-start.29
  9.6 5.7 %copy-start.21 = (bf16[512,512]{1,0:T(8,128)(2,1)S(1)}, bf16[512,512]{1,0:T(8,128)(2,1)}, u32[]{:S(2)}) copy-start(bf16[512,512]{1,0:T(8,128)(2,1)} %param.11) | copy-start | bytes 1572868
  9.6 0.5 copy-start.27
  12.9 7.0 %copy-start.24 = (f32[128]{0:T(128)S(1)}, f32[128]{0:T(128)}, u32[]{:S(2)}) copy-start(f32[128]{0:T(128)} %param.14) | copy-start | bytes 1540
  12.9 277.7 %reduce-scatter.2.cloned.1.call-start = ((), (), s32[]{:S(2)}) async-start(), calls=%async_computation.2 | async-start | bytes 6881280 | tf_op jit(solution)/shard_map/reduce_scatter | solution.py:390
  18.8 4.1 %copy-start.12 = (f32[512,4]{1,0:T(8,128)}, f32[512,4]{1,0:T(8,128)S(1)}, u32[]{:S(2)}) copy-start(f32[512,4]{1,0:T(8,128)S(1)} %copy.130) | copy-start | bytes 24580
  19.9 3.0 copy-start.5
  101.8 8.8 %copy-start.10 = (bf16[5376,256]{1,0:T(8,128)(2,1)S(1)}, bf16[5376,256]{1,0:T(8,128)(2,1)}, u32[]{:S(2)}) copy-start(bf16[5376,256]{1,0:T(8,128)(2,1)} %param.13) | copy-start | bytes 8257540
  104.0 0.7 copy-start.18
  104.0 1.6 copy-start.20
  105.6 18.3 %collective-permute-start.1 = (bf16[512,2,128]{2,0,1:T(8,128)(2,1)}, bf16[512,2,128]{2,0,1:T(8,128)(2,1)}, u32[]{:S(2)}, u32[]{:S(2)}) collective-permute-start(bf16[512,2,128]{2,0,1:T(8,128)(2,1)} %pad_maximum_fusion), channel_id=1, source_target_pairs={{0,4},{4,8},{8,12},{12,16},{16,20},{20,24},{24,28},{28,32},{32,36}... | collective-permute-start | bytes 786440 | tf_op jit(solution)/shard_map/ppermute | solution.py:19
  108.4 15.5 %collective-permute-start = (bf16[512,2,128]{2,0,1:T(8,128)(2,1)}, bf16[512,2,128]{2,0,1:T(8,128)(2,1)}, u32[]{:S(2)}, u32[]{:S(2)}) collective-permute-start(bf16[512,2,128]{2,0,1:T(8,128)(2,1)} %pad_maximum_fusion), channel_id=1, source_target_pairs={{0,8},{4,12},{8,16},{12,20},{16,24},{20,28},{24,32},{28,36},{32,40... | collective-permute-start | bytes 786440 | tf_op jit(solution)/shard_map/ppermute | solution.py:19
  117.4 11.6 %copy-start.9 = (pred[512,1536]{0,1:T(8,128)(4,1)S(1)}, pred[512,1536]{0,1:T(8,128)(4,1)}, u32[]{:S(2)}) copy-start(pred[512,1536]{0,1:T(8,128)(4,1)} %compare_and_fusion) | copy-start | bytes 2359300
  117.4 13.8 %collective-permute-start.3 = (bf16[512,2,128]{2,0,1:T(8,128)(2,1)}, bf16[512,2,128]{2,0,1:T(8,128)(2,1)S(1)}, u32[]{:S(2)}, u32[]{:S(2)}) collective-permute-start(bf16[512,2,128]{2,0,1:T(8,128)(2,1)} %copy.135), channel_id=1, source_target_pairs={{0,4},{4,8},{8,12},{12,16},{16,20},{20,24},{24,28},{28,32},{32,36}... | collective-permute-start | bytes 786440 | tf_op jit(solution)/shard_map/ppermute | solution.py:19
  121.2 12.5 %collective-permute-start.2 = (bf16[512,2,128]{2,0,1:T(8,128)(2,1)}, bf16[512,2,128]{2,0,1:T(8,128)(2,1)S(1)}, u32[]{:S(2)}, u32[]{:S(2)}) collective-permute-start(bf16[512,2,128]{2,0,1:T(8,128)(2,1)} %copy.135), channel_id=1, source_target_pairs={{0,8},{4,12},{8,16},{12,20},{16,24},{20,28},{24,32},{28,36},{32,40... | collective-permute-start | bytes 786440 | tf_op jit(solution)/shard_map/ppermute | solution.py:19
  129.0 4.7 %copy-start.15 = (bf16[512,512]{0,1:T(8,128)(2,1)S(1)}, bf16[512,512]{0,1:T(8,128)(2,1)}, u32[]{:S(2)}) copy-start(bf16[512,512]{0,1:T(8,128)(2,1)} %copy.138) | copy-start | bytes 1572868
  129.0 4.7 %copy-start.22 = (bf16[512,2,128]{2,0,1:T(8,128)(2,1)S(1)}, bf16[512,2,128]{2,0,1:T(8,128)(2,1)}, u32[]{:S(2)}) copy-start(bf16[512,2,128]{2,0,1:T(8,128)(2,1)} %copy.135) | copy-start | bytes 786436
  134.8 6.9 %copy-start.14 = (bf16[512,2,2,128]{3,0,2,1:T(8,128)(2,1)S(1)}, bf16[512,2,2,128]{3,0,2,1:T(8,128)(2,1)}, u32[]{:S(2)}) copy-start(bf16[512,2,2,128]{3,0,2,1:T(8,128)(2,1)} %fusion.13) | copy-start | bytes 1572868
  146.4 23.4 %collective-permute-start.4 = (bf16[512,2,128]{2,0,1:T(8,128)(2,1)S(1)}, bf16[512,2,128]{2,0,1:T(8,128)(2,1)S(1)}, u32[]{:S(2)}, u32[]{:S(2)}) collective-permute-start(bf16[512,2,128]{2,0,1:T(8,128)(2,1)S(1)} %get-tuple-element.20), channel_id=1, source_target_pairs={{4,0},{8,4},{12,8},{16,12},{20,16},{24,20},{28,24},{32,28},{36,32}... | collective-permute-start | bytes 786440 | tf_op jit(solution)/shard_map/ppermute | solution.py:19
  152.4 17.4 %collective-permute-start.5 = (bf16[512,2,128]{2,0,1:T(8,128)(2,1)S(1)}, bf16[512,2,128]{2,0,1:T(8,128)(2,1)S(1)}, u32[]{:S(2)}, u32[]{:S(2)}) collective-permute-start(bf16[512,2,128]{2,0,1:T(8,128)(2,1)S(1)} %get-tuple-element.21), channel_id=1, source_target_pairs={{8,0},{12,4},{16,8},{20,12},{24,16},{28,20},{32,24},{36,28},{40,32... | collective-permute-start | bytes 786440 | tf_op jit(solution)/shard_map/ppermute | solution.py:19
  157.7 12.1 %copy-start.6 = (f32[512,64]{1,0:T(8,128)S(1)}, f32[512,64]{1,0:T(8,128)}, u32[]{:S(2)}) copy-start(f32[512,64]{1,0:T(8,128)} %copy-done.5) | copy-start | bytes 393220
  157.7 12.4 %copy-start.26 = (f32[128]{0:T(128)S(1)}, f32[128]{0:T(128)}, u32[]{:S(2)}) copy-start(f32[128]{0:T(128)} %param.15) | copy-start | bytes 1540
  158.6 15.9 %collective-permute-start.6 = (bf16[512,2,128]{0,2,1:T(8,128)(2,1)}, bf16[512,2,128]{0,2,1:T(8,128)(2,1)}, u32[]{:S(2)}, u32[]{:S(2)}) collective-permute-start(bf16[512,2,128]{0,2,1:T(8,128)(2,1)} %get-tuple-element.18), channel_id=1, source_target_pairs={{4,0},{8,4},{12,8},{16,12},{20,16},{24,20},{28,24},{32,28},{36,32}... | collective-permute-start | bytes 786440 | tf_op jit(solution)/shard_map/ppermute | solution.py:19
  160.5 15.0 %collective-permute-start.7 = (bf16[512,2,128]{0,2,1:T(8,128)(2,1)}, bf16[512,2,128]{0,2,1:T(8,128)(2,1)}, u32[]{:S(2)}, u32[]{:S(2)}) collective-permute-start(bf16[512,2,128]{0,2,1:T(8,128)(2,1)} %get-tuple-element.19), channel_id=1, source_target_pairs={{8,0},{12,4},{16,8},{20,12},{24,16},{28,20},{32,24},{36,28},{40,32... | collective-permute-start | bytes 786440 | tf_op jit(solution)/shard_map/ppermute | solution.py:19
  172.8 4.7 %copy-start.11 = (bf16[5376,256]{1,0:T(8,128)(2,1)S(1)}, bf16[5376,256]{1,0:T(8,128)(2,1)}, u32[]{:S(2)}) copy-start(bf16[5376,256]{1,0:T(8,128)(2,1)} %param.13) | copy-start | bytes 8257540
  176.8 0.7 copy-start.16
  181.5 0.9 copy-start.19
  186.6 5.8 %copy-start.7 = (f32[512,64]{1,0:T(8,128)S(1)}, f32[512,64]{1,0:T(8,128)}, u32[]{:S(2)}) copy-start(f32[512,64]{1,0:T(8,128)} %copy-done.5) | copy-start | bytes 393220
  192.4 3.6 %copy-start.1 = (f32[512,4,128]{2,1,0:T(4,128)S(1)}, f32[512,4,128]{2,1,0:T(4,128)}, u32[]{:S(2)}) copy-start(f32[512,4,128]{2,1,0:T(4,128)} %reshape.249) | copy-start | bytes 3145732
  192.4 3.6 %copy-start.25 = (f32[128]{0:T(128)S(1)}, f32[128]{0:T(128)}, u32[]{:S(2)}) copy-start(f32[128]{0:T(128)} %param.14) | copy-start | bytes 1540
  194.6 1.0 copy-start.3
  194.7 1.3 copy-start.4
  194.7 4.8 %copy-start.13 = (f32[512,4]{1,0:T(8,128)S(1)}, f32[512,4]{1,0:T(8,128)}, u32[]{:S(2)}) copy-start(f32[512,4]{1,0:T(8,128)} %copy-done.12) | copy-start | bytes 24580
  197.9 6.8 %copy-start.17 = (bf16[512,2,128]{0,2,1:T(8,128)(2,1)S(1)}, bf16[512,2,128]{0,2,1:T(8,128)(2,1)}, u32[]{:S(2)}) copy-start(bf16[512,2,128]{0,2,1:T(8,128)(2,1)} %copy-done.16) | copy-start | bytes 786436
  203.8 6.1 %slice-start = ((s8[5505024]{0:T(1024)(128)(4,1)}), s8[4194304]{0:T(1024)(128)(4,1)S(1)}, s32[]{:S(2)}) async-start(s8[5505024]{0:T(1024)(128)(4,1)} %bitcast.88), calls=%async_computation.3 | async-start | bytes 8388608
  204.7 5.2 %slice-start.1 = ((s8[5505024]{0:T(1024)(128)(4,1)}), s8[1310720]{0:T(1024)(128)(4,1)S(1)}, s32[]{:S(2)}) async-start(s8[5505024]{0:T(1024)(128)(4,1)} %bitcast.88), calls=%async_computation.4 | async-start | bytes 2621440
  211.6 79.1 %copy-start.23 = (f32[5376]{0:T(1024)S(1)}, f32[5376]{0:T(1024)}, u32[]{:S(2)}) copy-start(f32[5376]{0:T(1024)} %param.10) | copy-start | bytes 64516
  287.3 5.8 %copy-start.30 = (f32[128]{0:T(128)S(1)}, f32[128]{0:T(128)}, u32[]{:S(2)}) copy-start(f32[128]{0:T(128)} %copy-done.29) | copy-start | bytes 1540
  287.3 5.8 %copy-start.28 = (f32[128]{0:T(128)S(1)}, f32[128]{0:T(128)}, u32[]{:S(2)}) copy-start(f32[128]{0:T(128)} %copy-done.27) | copy-start | bytes 1540
  290.6 2.5 copy-start.2
  290.6 2.6 copy-start.8
Sparse Core Ops, SparseCore 0:
  13.0 82.5 all-gather.1
  181.6 108.9 reduce-scatter.1

commit v2 on v1

--- a/solution.py
+++ b/solution.py
@@ -6,17 +6,12 @@
 from jax.sharding import PartitionSpec as P
 
 WINDOW = 1024
+WIDE = 4
 
 
 EPSILON = 1e-06
 QUERY_SCALE = 168.0 ** (-0.5)
 ROPE_BASE = 10000.0
-
-
-def from_behind(array, axis, by):
-    size = lax.axis_size(axis)
-    pairs = [(i, i + by) for i in range(size) if 0 <= i + by < size]
-    return lax.ppermute(array, axis, pairs)
 
 
 def doc_begin(doc_lengths, positions):
@@ -30,22 +25,14 @@
     return values * lax.rsqrt(jnp.mean(values * values, axis=1, keepdims=True) + EPSILON) * gain
 
 
-def head_norm(values, gain):
-    return values * lax.rsqrt(jnp.mean(values * values, axis=-1, keepdims=True) + EPSILON) * gain
-
-
-def rotate(values, positions):
-    half_size = values.shape[-1] // 2
-    powers = jnp.arange(half_size, dtype=jnp.float32) * (2.0 / values.shape[-1])
+def angle_tables(positions, head_size):
+    half_size = head_size // 2
+    powers = jnp.arange(half_size, dtype=jnp.float32) * (2.0 / head_size)
     frequency = ROPE_BASE ** (-powers)
     angles = positions.astype(jnp.float32)[:, None] * frequency[None, :]
-    cosine = jnp.cos(angles)[:, None, :]
-    sine = jnp.sin(angles)[:, None, :]
-    first = values[..., :half_size]
-    second = values[..., half_size:]
-    return jnp.concatenate(
-        [first * cosine - second * sine, second * cosine + first * sine], axis=-1
-    )
+    cosine = jnp.cos(angles)
+    sine = jnp.sin(angles)
+    return jnp.concatenate([cosine, cosine], axis=1), jnp.concatenate([-sine, sine], axis=1)
 
 
 def contract_last(left, right):
@@ -58,25 +45,6 @@
     return lax.dot_general(
         left, right, (((0,), (0,)), ((), ())), preferred_element_type=jnp.float32
     )
-
-
-def attend(queries, key_rows, value_rows, grads, lowest, positions, key_positions):
-    scores = jnp.einsum("qkgd,skd->kgqs", queries, key_rows, preferred_element_type=jnp.float32)
-    allowed = (key_positions[None, :] >= lowest[:, None]) & (
-        key_positions[None, :] <= positions[:, None]
-    )
-    exps = jnp.where(allowed[None, None], jnp.exp(scores), jnp.zeros_like(scores))
-    totals = jnp.sum(exps, axis=-1, keepdims=True)
-    probs = exps / totals
-    rounded = probs.astype(jnp.bfloat16)
-    outputs = jnp.einsum("kgqs,skd->qkgd", rounded, value_rows, preferred_element_type=jnp.float32)
-    deltas = jnp.sum(grads.astype(jnp.float32) * outputs, axis=-1)
-    along = jnp.einsum("qkgd,skd->kgqs", grads, value_rows, preferred_element_type=jnp.float32)
-    slopes = (probs * (along - jnp.transpose(deltas, (1, 2, 0))[..., None])).astype(jnp.bfloat16)
-    query_grad = jnp.einsum("kgqs,skd->qkgd", slopes, key_rows, preferred_element_type=jnp.float32)
-    key_grad = jnp.einsum("kgqs,qkgd->skd", slopes, queries, preferred_element_type=jnp.float32)
-    value_grad = jnp.einsum("kgqs,qkgd->skd", rounded, grads, preferred_element_type=jnp.float32)
-    return (query_grad, key_grad, value_grad)
 
 
 MESH_IDS = pl.DeviceIdType.MESH
@@ -312,80 +280,485 @@
     )(key_term, value_term)
 
 
+def turn(values, cosine, sine):
+    return values * cosine + pltpu.roll(values, values.shape[-1] // 2, 1) * sine
+
+
+def gather_kernel(
+    tokens_ref, gain_ref, raw_ref, q_gain_ref, k_gain_ref, cos_ref, sin_ref, w_key_ref, w_value_ref,
+    gathered_ref, query_ref, raw_key_ref, window_ref,
+    held, relay_up, relay_down, weights, window,
+    weight_sem, out_sem, window_sem, relay_send, relay_recv, cross_send, cross_recv,
+    pair_send, pair_recv, chunk_send, chunk_recv, halo_send, halo_recv,
+):
+    rows = tokens_ref.shape[0]
+    half = rows // 2
+    piece = half // 4
+    cols = w_key_ref.shape[1]
+    head_size = k_gain_ref.shape[1]
+    place = lax.axis_index("seq")
+    member = lax.axis_index("tp")
+    count = lax.axis_size("seq")
+    core = lax.rem(member, 2)
+    upper = member // 2
+    x = lax.rem(place, WIDE)
+    z = upper * 4 + lax.rem(place // WIDE, 4)
+    y = place // (4 * WIDE)
+
+    def along_z(by):
+        other = lax.rem(z + by, 8)
+        return ((y * 4 + lax.rem(other, 4)) * WIDE + x, other // 4 * 2 + core)
+
+    z_up, z_down = along_z(2), along_z(6)
+    partner = (place, upper * 2 + 1 - core)
+    later = [(lax.rem(place + by, count), member) for by in (1, 2)]
+    earlier = [(lax.rem(place + count - by, count), member) for by in (1, 2)]
+
+    def remote(source, target, send_sem, recv_sem, device):
+        return pltpu.make_async_remote_copy(
+            src_ref=source,
+            dst_ref=target,
+            send_sem=send_sem,
+            recv_sem=recv_sem,
+            device_id=device,
+            device_id_type=MESH_IDS,
+        )
+
+    loads = [
+        pltpu.make_async_copy(w_key_ref, weights.at[:, pl.ds(0, cols)], weight_sem.at[0]),
+        pltpu.make_async_copy(w_value_ref, weights.at[:, pl.ds(cols, cols)], weight_sem.at[1]),
+    ]
+    for one in loads:
+        one.start()
+    barrier = pltpu.get_barrier_semaphore()
+    for other in [z_up, z_down, partner] + later + earlier:
+        pl.semaphore_signal(barrier, inc=1, device_id=other, device_id_type=MESH_IDS)
+
+    own = pl.multiple_of(member * rows, rows)
+    beside = pl.multiple_of((upper * 2 + 1 - core) * rows, rows)
+    across = pl.multiple_of(((1 - upper) * 2 + core) * rows, rows)
+    corner = pl.multiple_of(((1 - upper) * 2 + 1 - core) * rows, rows)
+
+    def norm_rows(step, carry):
+        at = pl.ds(pl.multiple_of(step * 16, 16), 16)
+        values = tokens_ref[at, :].astype(jnp.float32)
+        scale = lax.rsqrt(jnp.mean(values * values, axis=1, keepdims=True) + EPSILON)
+        held[pl.ds(pl.multiple_of(own + step * 16, 16), 16), :] = (
+            values * scale * gain_ref[...]
+        ).astype(jnp.bfloat16)
+        return carry
+
+    lax.fori_loop(0, rows // 16, norm_rows, 0)
+    pl.semaphore_wait(barrier, 7)
+
+    to_partner = remote(
+        held.at[pl.ds(own, rows)], held.at[pl.ds(own, rows)], pair_send.at[0], pair_recv.at[0], partner
+    )
+    to_partner.start()
+
+    def first_up(step):
+        return remote(
+            held.at[pl.ds(pl.multiple_of(own + step * piece, piece), piece)],
+            relay_up.at[pl.ds(pl.multiple_of(step * piece, piece), piece)],
+            relay_send.at[0, step], relay_recv.at[0, step], z_up,
+        )
+
+    def first_down(step):
+        return remote(
+            held.at[pl.ds(pl.multiple_of(own + half + step * piece, piece), piece)],
+            relay_down.at[pl.ds(pl.multiple_of(step * piece, piece), piece)],
+            relay_send.at[1, step], relay_recv.at[1, step], z_down,
+        )
+
+    def second_up(step):
+        target = pl.multiple_of(((1 - lax.rem(z + 2, 8) // 4) * 2 + core) * rows + step * piece, piece)
+        return remote(
+            relay_up.at[pl.ds(pl.multiple_of(step * piece, piece), piece)],
+            held.at[pl.ds(target, piece)],
+            cross_send.at[0, step], cross_recv.at[0, step], z_up,
+        )
+
+    def second_down(step):
+        target = pl.multiple_of(
+            ((1 - lax.rem(z + 6, 8) // 4) * 2 + core) * rows + half + step * piece, piece
+        )
+        return remote(
+            relay_down.at[pl.ds(pl.multiple_of(step * piece, piece), piece)],
+            held.at[pl.ds(target, piece)],
+            cross_send.at[1, step], cross_recv.at[1, step], z_down,
+        )
+
+    def pass_on(side, step):
+        at = pl.ds(pl.multiple_of(across + side * half + step * piece, piece), piece)
+        return remote(held.at[at], held.at[at], chunk_send.at[side, step], chunk_recv.at[side, step], partner)
+
+    for step in range(4):
+        first_up(step).start()
+        first_down(step).start()
+
+    def halo(by, index, begin, size):
+        return remote(
+            window.at[2, pl.ds(begin, size)],
+            window.at[2 - by, pl.ds(begin, size)],
+            halo_send.at[by - 1, index], halo_recv.at[by - 1, index], later[by - 1],
+        )
+
+    def project(parts):
+        block = [held[pl.ds(begin, size), :] for begin, size in parts]
+        block = block[0] if len(block) == 1 else jnp.concatenate(block, axis=0)
+        result = jnp.dot(block, weights[...], preferred_element_type=jnp.float32)
+        at = 0
+        for begin, size in parts:
+            mine = result[at : at + size]
+            at += size
+            where = pl.ds(begin, size)
+            raw_key_ref[where, :] = mine[:, :cols]
+            window[2, where, cols:] = mine[:, cols:].astype(jnp.bfloat16)
+            for head in range(cols // head_size):
+                lanes = slice(head * head_size, (head + 1) * head_size)
+                values = mine[:, lanes]
+                scale = lax.rsqrt(jnp.mean(values * values, axis=1, keepdims=True) + EPSILON)
+                values = values * scale * k_gain_ref[...]
+                window[2, where, lanes] = turn(values, cos_ref[where, :], sin_ref[where, :]).astype(
+                    jnp.bfloat16
+                )
+
+    out_own = pltpu.make_async_copy(
+        held.at[pl.ds(own, rows)], gathered_ref.at[pl.ds(own, rows)], out_sem.at[0]
+    )
+    out_own.start()
+    for one in loads:
+        one.wait()
+    project([(own, rows)])
+    halo(1, 0, own, rows).start()
+    halo(2, 0, own, rows).start()
+    to_partner.wait_recv()
+    out_beside = pltpu.make_async_copy(
+        held.at[pl.ds(beside, rows)], gathered_ref.at[pl.ds(beside, rows)], out_sem.at[1]
+    )
+    out_beside.start()
+    project([(beside, rows)])
+    halo(1, 1, beside, rows).start()
+    halo(2, 1, beside, rows).start()
+
+    for head in range(raw_ref.shape[1] // head_size):
+        lanes = slice(head * head_size, (head + 1) * head_size)
+        values = raw_ref[:, lanes].astype(jnp.float32)
+        scale = lax.rsqrt(jnp.mean(values * values, axis=1, keepdims=True) + EPSILON)
+        values = values * scale * q_gain_ref[...]
+        query_ref[:, lanes] = (turn(values, cos_ref[...], sin_ref[...]) * QUERY_SCALE).astype(
+            jnp.bfloat16
+        )
+
+    for step in range(4):
+        first_up(step).wait_recv()
+        second_up(step).start()
+        first_down(step).wait_recv()
+        second_down(step).start()
+
+    def groups(step):
+        return [
+            (pl.multiple_of(base + side * half + step * piece, piece), piece)
+            for base in (across, corner)
+            for side in (0, 1)
+        ]
+
+    def arrive(step, carry):
+        for side, copy in ((0, second_up(step)), (1, second_down(step))):
+            copy.wait_recv()
+            pass_on(side, step).start()
+        for side in (0, 1):
+            pass_on(side, step).wait_recv()
+        project(groups(step))
+        for index, (begin, size) in enumerate(groups(step)):
+            halo(1, 2 + step * 4 + index, begin, size).start()
+            halo(2, 2 + step * 4 + index, begin, size).start()
+        return carry
+
+    lax.fori_loop(0, 4, arrive, 0)
+    out_across = pltpu.make_async_copy(
+        held.at[pl.ds(across, rows)], gathered_ref.at[pl.ds(across, rows)], out_sem.at[2]
+    )
+    out_corner = pltpu.make_async_copy(
+        held.at[pl.ds(corner, rows)], gathered_ref.at[pl.ds(corner, rows)], out_sem.at[3]
+    )
+    out_across.start()
+    out_corner.start()
+
+    def each_halo(act):
+        for by in (1, 2):
+            act(halo(by, 0, own, rows))
+            act(halo(by, 1, beside, rows))
+
+            def inner(step, carry):
+                for index, (begin, size) in enumerate(groups(step)):
+                    act(halo(by, 2 + step * 4 + index, begin, size))
+                return carry
+
+            lax.fori_loop(0, 4, inner, 0)
+
+    each_halo(lambda copy: copy.wait_recv())
+    out_window = pltpu.make_async_copy(window, window_ref, window_sem.at[0])
+    out_window.start()
+    each_halo(lambda copy: copy.wait_send())
+    to_partner.wait_send()
+    for step in range(4):
+        first_up(step).wait_send()
+        first_down(step).wait_send()
+        second_up(step).wait_send()
+        second_down(step).wait_send()
+        pass_on(0, step).wait_send()
+        pass_on(1, step).wait_send()
+    for one in (out_own, out_beside, out_across, out_corner, out_window):
+        one.wait()
+
+
+def gather_and_project(tokens, in_gain, raw_queries, w_key, w_value, q_gain, k_gain, cosine, sine):
+    rows, depth = tokens.shape
+    shard = rows * 4
+    cols = w_key.shape[1]
+    bf = jnp.bfloat16
+    vmem = pl.BlockSpec(memory_space=pltpu.VMEM)
+    anywhere = pl.BlockSpec(memory_space=pl.ANY)
+    dma = pltpu.SemaphoreType.DMA
+    return pl.pallas_call(
+        gather_kernel,
+        out_shape=[
+            jax.ShapeDtypeStruct((shard, depth), bf),
+            jax.ShapeDtypeStruct(raw_queries.shape, bf),
+            jax.ShapeDtypeStruct((shard, cols), jnp.float32),
+            jax.ShapeDtypeStruct((3, shard, 2 * cols), bf),
+        ],
+        in_specs=[vmem] * 7 + [anywhere] * 2,
+        out_specs=[anywhere, vmem, vmem, anywhere],
+        scratch_shapes=[
+            pltpu.VMEM((shard, depth), bf),
+            pltpu.VMEM((rows // 2, depth), bf),
+            pltpu.VMEM((rows // 2, depth), bf),
+            pltpu.VMEM((depth, 2 * cols), bf),
+            pltpu.VMEM((3, shard, 2 * cols), bf),
+            dma((2,)),
+            dma((4,)),
+            dma((1,)),
+            dma((2, 4)),
+            dma((2, 4)),
+            dma((2, 4)),
+            dma((2, 4)),
+            dma((1,)),
+            dma((1,)),
+            dma((2, 4)),
+            dma((2, 4)),
+            dma((2, 18)),
+            dma((2, 18)),
+        ],
+        compiler_params=pltpu.CompilerParams(
+            collective_id=2, has_side_effects=True, vmem_limit_bytes=40 * 1024 * 1024
+        ),
+        cost_estimate=pl.CostEstimate(
+            flops=3_000_000_000, bytes_accessed=150_000_000, transcendentals=0
+        ),
+        name="gather_and_project",
+    )(tokens, in_gain[None, :], raw_queries, q_gain[None, :], k_gain[None, :], cosine, sine, w_key, w_value)
+
+
+def unturn(values, cosine, sine):
+    return values * cosine - pltpu.roll(values, values.shape[-1] // 2, 1) * sine
+
+
+def norm_back(grad, values, gain):
+    scale = lax.rsqrt(jnp.mean(values * values, axis=1, keepdims=True) + EPSILON)
+    unit = values * scale
+    inner = grad * gain
+    return scale * (inner - unit * jnp.mean(inner * unit, axis=1, keepdims=True))
+
+
+def attend_kernel(
+    query_ref, window_ref, out_grad_ref, low_ref, raw_ref, raw_key_ref, cos_ref, sin_ref, q_gain_ref, k_gain_ref,
+    grad_query_ref, grad_kv_ref,
+    exps, along, totals, query_total, parts, returned,
+    send_sem, recv_sem,
+):
+    shard = query_ref.shape[0]
+    head_size = q_gain_ref.shape[1]
+    kv_heads = raw_key_ref.shape[1] // head_size
+    group_size = query_ref.shape[1] // raw_key_ref.shape[1]
+    tile = shard // 2
+    reach = 2 * shard
+    place = lax.axis_index("seq")
+    member = lax.axis_index("tp")
+    count = lax.axis_size("seq")
+    later = [(lax.rem(place + by, count), member) for by in (2, 1)]
+    earlier = [(lax.rem(place + count - by, count), member) for by in (2, 1)]
+    barrier = pltpu.get_barrier_semaphore()
+    for other in later + earlier:
+        pl.semaphore_signal(barrier, inc=1, device_id=other, device_id_type=MESH_IDS)
+
+    totals[...] = jnp.zeros_like(totals)
+
+    def across(left, right):
+        return lax.dot_general(left, right, (((1,), (1,)), ((), ())), preferred_element_type=jnp.float32)
+
+    def back(window, head):
+        return pltpu.make_async_remote_copy(
+            src_ref=parts.at[window, head],
+            dst_ref=returned.at[window, head],
+            send_sem=send_sem.at[window, head],
+            recv_sem=recv_sem.at[window, head],
+            device_id=earlier[window],
+            device_id_type=MESH_IDS,
+        )
+
+    for head in range(kv_heads):
+        key_lanes = slice(head * head_size, (head + 1) * head_size)
+        value_lanes = slice((kv_heads + head) * head_size, (kv_heads + head + 1) * head_size)
+        lanes = [
+            slice((head * group_size + member_of) * head_size, (head * group_size + member_of + 1) * head_size)
+            for member_of in range(group_size)
+        ]
+
+        def half(step, carry):
+            begin = pl.multiple_of(step * tile, tile)
+            rows = pl.ds(begin, tile)
+            queries = jnp.concatenate([query_ref[rows, at] for at in lanes], axis=0)
+            grads = jnp.concatenate([out_grad_ref[rows, at] for at in lanes], axis=0)
+            low = low_ref[step]
+            low = jnp.concatenate([low] * group_size, axis=1)
+            width = group_size * tile
+            high = lax.broadcasted_iota(jnp.int32, (1, tile), 1) + (reach + begin)
+            high = jnp.concatenate([high] * group_size, axis=1)
+
+            def scores(index, stats):
+                total, delta = stats
+                first = pl.multiple_of(begin + index * tile, tile)
+                key_rows = pl.ds(first, tile)
+                score = across(window_ref[key_rows, key_lanes], queries)
+                partial = across(window_ref[key_rows, value_lanes], grads)
+                key = lax.broadcasted_iota(jnp.int32, (tile, width), 0) + first
+                value = jnp.where((key >= low) & (key <= high), jnp.exp(score), 0.0)
+                at = pl.ds(pl.multiple_of(index * tile, tile), tile)
+                exps[at, :] = value
+                along[at, :] = partial
+                total = total + jnp.sum(value, axis=0, keepdims=True)
+                delta = delta + jnp.sum(value * partial, axis=0, keepdims=True)
+                return total, delta
+
+            nothing = jnp.zeros((1, width), jnp.float32)
+            total, delta = lax.fori_loop(0, reach // tile + 1, scores, (nothing, nothing))
+            inverse = 1.0 / total
+            delta = delta * inverse
+            query_total[...] = jnp.zeros_like(query_total)
+
+            def slopes(index, carry):
+                key_rows = pl.ds(pl.multiple_of(begin + index * tile, tile), tile)
+                at = pl.ds(pl.multiple_of(index * tile, tile), tile)
+                probs = exps[at, :] * inverse
+                slope = (probs * (along[at, :] - delta)).astype(jnp.bfloat16)
+                query_total[...] += contract_first(window_ref[key_rows, key_lanes], slope)
+                totals[key_rows, key_lanes] += jnp.dot(slope, queries, preferred_element_type=jnp.float32)
+                totals[key_rows, value_lanes] += jnp.dot(
+                    probs.astype(jnp.bfloat16), grads, preferred_element_type=jnp.float32
+                )
+                return carry
+
+            lax.fori_loop(0, reach // tile + 1, slopes, 0)
+            flipped = query_total[...].T
+            for member_of, at in enumerate(lanes):
+                grad = flipped[member_of * tile : (member_of + 1) * tile] * QUERY_SCALE
+                grad = unturn(grad, cos_ref[rows, :], sin_ref[rows, :])
+                values = raw_ref[rows, at].astype(jnp.float32)
+                grad_query_ref[rows, at] = norm_back(grad, values, q_gain_ref[...]).astype(jnp.bfloat16)
+            return carry
+
+        lax.fori_loop(0, 2, half, 0)
+        for window in range(2):
+            rows = slice(window * shard, (window + 1) * shard)
+            parts[window, head, :, :head_size] = totals[rows, key_lanes].astype(jnp.bfloat16)
+            parts[window, head, :, head_size:] = totals[rows, value_lanes].astype(jnp.bfloat16)
+        if head == 0:
+            pl.semaphore_wait(barrier, 4)
+        for window in range(2):
+            back(window, head).start()
+
+    own = slice(reach, reach + shard)
+    for head in range(kv_heads):
+        key_lanes = slice(head * head_size, (head + 1) * head_size)
+        value_lanes = slice((kv_heads + head) * head_size, (kv_heads + head + 1) * head_size)
+        for window in range(2):
+            back(window, head).wait_recv()
+        key_grad = totals[own, key_lanes]
+        value_grad = totals[own, value_lanes]
+        for window in (1, 0):
+            key_grad = key_grad + returned[window, head, :, :head_size].astype(jnp.float32)
+            value_grad = value_grad + returned[window, head, :, head_size:].astype(jnp.float32)
+        grad_kv_ref[:, value_lanes] = value_grad.astype(jnp.bfloat16)
+        key_grad = unturn(key_grad, cos_ref[...], sin_ref[...])
+        grad_kv_ref[:, key_lanes] = norm_back(key_grad, raw_key_ref[:, key_lanes], k_gain_ref[...]).astype(
+            jnp.bfloat16
+        )
+    for head in range(kv_heads):
+        for window in range(2):
+            back(window, head).wait_send()
+
+
+def attend_back(query_rot, window, out_grad, low, raw_queries, raw_keys, cosine, sine, q_gain, k_gain):
+    shard = query_rot.shape[0]
+    head_size = q_gain.shape[0]
+    kv_heads = raw_keys.shape[1] // head_size
+    group_size = query_rot.shape[1] // raw_keys.shape[1]
+    tile = shard // 2
+    width = group_size * tile
+    vmem = pl.BlockSpec(memory_space=pltpu.VMEM)
+    return pl.pallas_call(
+        attend_kernel,
+        out_shape=[
+            jax.ShapeDtypeStruct(query_rot.shape, jnp.bfloat16),
+            jax.ShapeDtypeStruct((shard, 2 * raw_keys.shape[1]), jnp.bfloat16),
+        ],
+        in_specs=[vmem] * 10,
+        out_specs=[vmem] * 2,
+        scratch_shapes=[
+            pltpu.VMEM((2 * shard + tile, width), jnp.float32),
+            pltpu.VMEM((2 * shard + tile, width), jnp.float32),
+            pltpu.VMEM((3 * shard, 2 * raw_keys.shape[1]), jnp.float32),
+            pltpu.VMEM((head_size, width), jnp.float32),
+            pltpu.VMEM((2, kv_heads, shard, 2 * head_size), jnp.bfloat16),
+            pltpu.VMEM((2, kv_heads, shard, 2 * head_size), jnp.bfloat16),
+            pltpu.SemaphoreType.DMA((2, kv_heads)),
+            pltpu.SemaphoreType.DMA((2, kv_heads)),
+        ],
+        compiler_params=pltpu.CompilerParams(
+            collective_id=3, has_side_effects=True, vmem_limit_bytes=40 * 1024 * 1024
+        ),
+        cost_estimate=pl.CostEstimate(
+            flops=8_000_000_000, bytes_accessed=100_000_000, transcendentals=3_000_000
+        ),
+        name="attend_back",
+    )(
+        query_rot, window.reshape(3 * shard, window.shape[2]), out_grad, low, raw_queries, raw_keys,
+        cosine, sine, q_gain[None, :], k_gain[None, :],
+    )
+
+
 def shards(tokens, in_gain, raw_queries, w_key, w_value, q_gain, k_gain, doc_lengths, out_grad):
-    tp_count = lax.axis_size("tp")
     head_size = q_gain.shape[0]
-    kv_heads = w_key.shape[1] // head_size
-    group_size = raw_queries.shape[1] // w_key.shape[1]
-    shard_rows = tokens.shape[0] * tp_count
-    reach_count = (WINDOW - 2) // shard_rows + 1
+    shard_rows = tokens.shape[0] * lax.axis_size("tp")
+    reach = 2 * shard_rows
     x_float = tokens.astype(jnp.float32)
-    normed_rows = input_norm(x_float, in_gain).astype(jnp.bfloat16)
-    gathered = lax.all_gather(normed_rows, "tp", axis=0, tiled=True)
     first_row = lax.axis_index("seq") * shard_rows
     positions = first_row + jnp.arange(shard_rows, dtype=jnp.int32)
     begins = doc_begin(doc_lengths, positions)
-    offsets = positions - begins
     lowest = jnp.maximum(begins, positions - (WINDOW - 1))
-    queries = raw_queries.astype(jnp.float32).reshape(shard_rows, -1, head_size)
-    keys_raw = jnp.dot(gathered, w_key, preferred_element_type=jnp.float32).reshape(
-        shard_rows, -1, head_size
-    )
-    values_raw = jnp.dot(gathered, w_value, preferred_element_type=jnp.float32).reshape(
-        shard_rows, -1, head_size
-    )
-
-    def query_map(values):
-        return rotate(head_norm(values, q_gain), offsets) * QUERY_SCALE
-
-    def key_map(values):
-        return rotate(head_norm(values, k_gain), offsets)
-
-    query_rot, query_back = jax.vjp(query_map, queries)
-    key_rot, key_back = jax.vjp(key_map, keys_raw)
-    query_rows = query_rot.astype(jnp.bfloat16).reshape(shard_rows, kv_heads, group_size, head_size)
-    key_rows = key_rot.astype(jnp.bfloat16)
-    value_rows = values_raw.astype(jnp.bfloat16)
-    grad_rows = out_grad.reshape(shard_rows, kv_heads, group_size, head_size)
-    rim_keys = []
-    rim_values = []
-    for distance in range(reach_count, 0, -1):
-        far_keys, far_values = from_behind((key_rows, value_rows), "seq", distance)
-        rim_keys.append(far_keys)
-        rim_values.append(far_values)
-    key_window = jnp.concatenate(rim_keys + [key_rows], axis=0)
-    value_window = jnp.concatenate(rim_values + [value_rows], axis=0)
-    key_positions = (
-        first_row
-        - reach_count * shard_rows
-        + jnp.arange((reach_count + 1) * shard_rows, dtype=jnp.int32)
-    )
-    query_grad, key_grad_all, value_grad_all = attend(
-        query_rows, key_window, value_window, grad_rows, lowest, positions, key_positions
-    )
-    own_start = reach_count * shard_rows
-    key_grad = key_grad_all[own_start:]
-    value_grad = value_grad_all[own_start:]
-    for distance in range(1, reach_count + 1):
-        lower_row = (reach_count - distance) * shard_rows
-        back_keys, back_values = (
-            from_behind(
-                key_grad_all[lower_row : lower_row + shard_rows].astype(jnp.bfloat16),
-                "seq",
-                -distance,
-            ).astype(jnp.float32),
-            from_behind(
-                value_grad_all[lower_row : lower_row + shard_rows].astype(jnp.bfloat16),
-                "seq",
-                -distance,
-            ).astype(jnp.float32),
-        )
-        key_grad = key_grad + back_keys
-        value_grad = value_grad + back_values
-    query_grad = query_grad.reshape(shard_rows, kv_heads * group_size, head_size)
-    grad_queries = query_back(query_grad)[0].reshape(shard_rows, -1).astype(jnp.bfloat16)
-    grad_k = key_back(key_grad)[0].reshape(shard_rows, -1).astype(jnp.bfloat16)
-    grad_v = value_grad.reshape(shard_rows, -1).astype(jnp.bfloat16)
+    low = (lowest - (first_row - reach)).reshape(2, 1, shard_rows // 2)
+    cosine, sine = angle_tables(positions - begins, head_size)
+    gathered, query_rot, raw_keys, window = gather_and_project(
+        tokens, in_gain, raw_queries, w_key, w_value, q_gain, k_gain, cosine, sine
+    )
+    grad_queries, grad_kv = attend_back(
+        query_rot, window, out_grad, low, raw_queries, raw_keys, cosine, sine, q_gain, k_gain
+    )
+    kv_cols = w_key.shape[1]
+    grad_k = grad_kv[:, :kv_cols]
+    grad_v = grad_kv[:, kv_cols:]
     partial_sum = contract_last(grad_k, w_key) + contract_last(grad_v, w_value)
     normed_grad = lax.psum_scatter(
         partial_sum.astype(jnp.bfloat16), "tp", scatter_dimension=0, tiled=True
@@ -394,8 +767,8 @@
     def norm_map(values):
         return input_norm(values, in_gain)
 
-    unused_rows, norm_back = jax.vjp(norm_map, x_float)
-    grad_x = norm_back(normed_grad)[0].astype(jnp.bfloat16)
+    unused_rows, input_back = jax.vjp(norm_map, x_float)
+    grad_x = input_back(normed_grad)[0].astype(jnp.bfloat16)
     key_term = contract_first(gathered, grad_k)
     value_term = contract_first(gathered, grad_v).astype(jnp.bfloat16)
     grad_wk, grad_wv = weight_sum(key_term, value_term)

time: 306 us -> 271 us (0.89)
  Pallas kernels: 75.7 us -> 221 us
  waiting for transfers between devices: 76.7 us -> 1.85 us
  matrix products: 47.5 us -> 14.3 us
  starting transfers between devices: 30.8 us -> 0.04 us
  other arithmetic: 34.4 us -> 6.14 us
  local copies, waits for them, and re-layouts: 23.3 us -> 11 us
    pallas_call x0 -> x2, Pallas kernels: none -> 123 us  [the longest x1 81.3 us: gather_and_project(): pl.pallas_call(gather_kernel, out_shape=[jax.ShapeDtypeStruct((shard, dep...]
    all_gather x1 -> x0, waiting for transfers between devices: 69.8 us -> none  [shards(): gathered = lax.all_gather(normed_rows, 'tp', axis=0, tiled=True)]
    dot_general x8 -> x0, matrix products: 35 us -> none  [the longest x1 6.88 us: attend(): jnp.einsum('qkgd,skd->kgqs', grads, value_rows, preferred_element_type=jn...]
    ppermute x8 -> x0, starting transfers between devices: 30.7 us -> none  [from_behind(): return lax.ppermute(array, axis, pairs)]
    pallas_call x1, Pallas kernels: 75.7 us -> 98 us  [weight_sum(): pl.pallas_call(weight_sum_kernel, out_shape=[jax.ShapeDtypeStruct((rows,...]
    convert_element_type x7 -> x2, other arithmetic: 14.7 us -> 1.82 us  [the longest x1 1.81 us: shards(): grad_x = input_back(normed_grad)[0].astype(jnp.bfloat16)]
    reduce_sum x4 -> x0, other arithmetic: 5.84 us -> none  [the longest x1 2.43 us: input_norm(): values * lax.rsqrt(jnp.mean(values * values, axis=1, keepdims=True) + EPS...]
    unnamed x74 -> x33, local copies, waits for them, and re-layouts: 13.8 us -> 9.49 us
  transfers between devices with their start and end apart: 10 -> 1, of which waited for: 4 -> 1; matrix products, arithmetic and copies ran while one was open for 21% -> 3% of each run, Pallas kernels for 25% -> 36%
where the time goes in v2:
time: 271 us; the launch traced here: 269 us
  Pallas kernels  221 us (82%)
  matrix products  14.3 us (5%)
  between operations  14.2 us (5%)
  local copies, waits for them, and re-layouts  11 us (4%)
  other arithmetic  6.14 us (2%)
    pallas_call x1, Pallas kernels, weight_sum(): pl.pallas_call(weight_sum_kernel, out_shape=[jax.ShapeDtypeStruct((rows,...  98 us
    pallas_call x1, Pallas kernels, gather_and_project(): pl.pallas_call(gather_kernel, out_shape=[jax.ShapeDtypeStruct((shard, dep...  81.3 us
    pallas_call x1, Pallas kernels, attend_back(): pl.pallas_call(attend_kernel, out_shape=[jax.ShapeDtypeStruct(query_rot.s...  41.9 us
    unnamed x33, local copies, waits for them, and re-layouts  9.49 us
    dot_general x2, matrix products, contract_first(): lax.dot_general(left, right, (((0,), (0,)), ((), ())), preferred_element_...  8.41 us
    dot_general x2, matrix products, contract_last(): lax.dot_general(left, right, (((1,), (1,)), ((), ())), preferred_element_...  5.85 us
  transfers between devices with their start and end apart: 1, of which 1 were waited for; matrix products, arithmetic and copies ran while one was open for 3% of the time, Pallas kernels for 36%

profile of v2, /device:TPU:61, one launch (start us, length us, event | category | flops | bytes accessed | tf_op | source)
XLA Modules:
  0.0 268.7 jit_solution(13448522850915212661)
XLA Ops:
  7.2 0.0 reduce-scatter.2.cloned.1.call-start
  7.2 0.7 copy.15
  8.0 0.1 reduce-window.9
  8.0 0.1 reduce
  8.2 0.7 sub.30
  8.8 0.1 select_reduce_fusion
  8.9 0.8 broadcast_in_dim.22.gain_ref
  9.7 1.0 fusion.9
  10.7 0.2 pad_maximum_fusion
  10.9 0.0 copy-start
  10.9 1.3 copy-done
  12.2 0.0 copy-start.2
  12.3 1.8 copy-done.2
  14.0 0.0 copy-start.4
  14.0 1.8 copy-done.4
  15.8 0.0 copy-start.6
  15.8 1.0 copy-done.6
  16.8 0.0 copy-start.9
  16.9 0.7 copy-done.9
  17.5 0.0 copy-start.11
  17.5 0.7 copy-done.11
  18.2 81.3 %gather_and_project.1 = (bf16[512,5376]{1,0:T(8,128)(2,1)}, bf16[512,512]{1,0:T(8,128)(2,1)S(1)}, f32[512,256]{1,0:T(8,128)S(1)}, bf16[3,512,512]{2,1,0:T(8,128)(2,1)S(1)}) custom-call(bf16[128,5376]{1,0:T(8,128)(2,1)S(1)} %copy-done, f32[1,5376]{1,0:T(1,128)S(1)} %broadcast_in_dim.22.gain_ref, bf16[512,512]{1,0:T(8,128)(2,1)S(1)} %copy-done.6, ...), custom_call_target="tpu_custom_call" | custom-call | flops 3000000000 | bytes 150000000 | tf_op jit(solution)/shard_map/gather_and_project/pallas_call | solution.py:524
  99.5 0.0 copy-done.7
  99.5 0.0 copy-done.8
  99.5 0.0 copy-done.10
  99.5 0.0 copy-done.12
  99.5 0.0 copy-start.5
  99.5 41.9 %attend_back.1 = (bf16[512,512]{1,0:T(8,128)(2,1)S(1)}, bf16[512,512]{1,0:T(8,128)(2,1)S(1)}) custom-call(bf16[512,512]{1,0:T(8,128)(2,1)S(1)} %get-tuple-element.12.query_ref, bf16[1536,512]{1,0:T(8,128)(2,1)S(1)} %bitcast.13, bf16[512,512]{1,0:T(8,128)(2,1)S(1)} %copy-done.8, s32[2,1,256]{2,1,0:T(1,128)S(1)} %maximum_subtract_fusion.low_ref, ...), custom_call_target="tpu_custom_call" | custom-call | flops 8000000000 | bytes 100000000 | tf_op jit(solution)/shard_map/attend_back/pallas_call | solution.py:711
  141.4 0.0 copy-done.5
  141.4 0.0 copy-start.3
  141.4 1.6 fusion.7
  143.1 0.1 copy-done.3
  143.2 4.2 %add_convert_fusion = bf16[512,5376]{1,0:T(8,128)(2,1)} fusion(f32[512,5376]{1,0:T(8,128)S(1)} %fusion.7, bf16[5376,256]{1,0:T(8,128)(2,1)S(1)} %copy-done.3, bf16[512,512]{1,0:T(8,128)(2,1)S(1)} %get-tuple-element.15), kind=kOutput, calls=%fused_computation | convolution fusion | flops 1414791168 | bytes 19529728 | tf_op jit(solution)/shard_map/dot_general | solution.py:39
  147.4 0.0 reduce-scatter.2.cloned.1.call-update
  147.5 4.2 %fusion.5.key_ref = f32[5376,256]{1,0:T(8,128)S(1)} fusion(bf16[512,5376]{1,0:T(8,128)(2,1)} %get-tuple-element.17, bf16[512,512]{1,0:T(8,128)(2,1)S(1)} %get-tuple-element.15), kind=kOutput, calls=%fused_computation.16 | convolution fusion | flops 1409286144 | bytes 11272192 | tf_op jit(solution)/shard_map/dot_general | solution.py:45
  151.7 4.2 %convolution_convert_fusion.value_ref = bf16[5376,256]{1,0:T(8,128)(2,1)S(1)} fusion(bf16[512,5376]{1,0:T(8,128)(2,1)} %get-tuple-element.17, bf16[512,512]{1,0:T(8,128)(2,1)S(1)} %get-tuple-element.15), kind=kOutput, calls=%fused_computation.1 | convolution fusion | flops 1410662400 | bytes 8519680 | tf_op jit(solution)/shard_map/dot_general | solution.py:45
  155.9 0.0 copy-start.1
  155.9 0.0 copy-start.14
  155.9 98.0 %weight_sum.1 = (f32[84,256]{1,0:T(8,128)S(1)}, f32[84,256]{1,0:T(8,128)S(1)}) custom-call(f32[5376,256]{1,0:T(8,128)S(1)} %fusion.5.key_ref, bf16[5376,256]{1,0:T(8,128)(2,1)S(1)} %convolution_convert_fusion.value_ref), custom_call_target="tpu_custom_call" | custom-call | flops 100000000 | bytes 150000000 | tf_op jit(solution)/shard_map/weight_sum/pallas_call | solution.py:253
  254.0 1.8 reduce-scatter.2.cloned.1.call-done
  255.8 0.0 copy-done.1
  255.8 0.0 copy-done.14
  255.8 2.2 fusion
  258.0 0.0 copy-done.13
  258.0 1.8 fusion.2
  259.8 0.8 copy.19
  260.6 0.6 copy.20
  261.2 0.6 copy.21
  (10 shorter events, 0.1 us)
Async XLA Ops:
  7.2 248.6 %reduce-scatter.2.cloned.1.call-start = ((), (), s32[]{:S(2)}) async-start(), calls=%async_computation.1 | async-start | bytes 6881280 | tf_op jit(solution)/shard_map/reduce_scatter | solution.py:763
  10.9 1.3 copy-start
  12.2 1.8 copy-start.2
  14.0 1.8 copy-start.4
  15.8 1.0 copy-start.6
  16.8 0.7 copy-start.9
  17.5 0.7 copy-start.11
  18.2 81.3 %copy-start.7 = (bf16[512,512]{1,0:T(8,128)(2,1)S(1)}, bf16[512,512]{1,0:T(8,128)(2,1)}, u32[]{:S(2)}) copy-start(bf16[512,512]{1,0:T(8,128)(2,1)} %raw_ref.3) | copy-start | bytes 1572868
  18.2 81.3 %copy-start.8 = (bf16[512,512]{1,0:T(8,128)(2,1)S(1)}, bf16[512,512]{1,0:T(8,128)(2,1)}, u32[]{:S(2)}) copy-start(bf16[512,512]{1,0:T(8,128)(2,1)} %out_grad_ref.1) | copy-start | bytes 1572868
  18.2 81.3 %copy-start.10 = (f32[128]{0:T(128)S(1)}, f32[128]{0:T(128)}, u32[]{:S(2)}) copy-start(f32[128]{0:T(128)} %param.14) | copy-start | bytes 1540
  18.2 81.3 %copy-start.12 = (f32[128]{0:T(128)S(1)}, f32[128]{0:T(128)}, u32[]{:S(2)}) copy-start(f32[128]{0:T(128)} %param.15) | copy-start | bytes 1540
  99.5 41.9 %copy-start.5 = (bf16[5376,256]{1,0:T(8,128)(2,1)S(1)}, bf16[5376,256]{1,0:T(8,128)(2,1)}, u32[]{:S(2)}) copy-start(bf16[5376,256]{1,0:T(8,128)(2,1)} %w_key_ref.1) | copy-start | bytes 8257540
  141.4 1.8 copy-start.3
  155.9 99.9 %copy-start.1 = (bf16[128,5376]{1,0:T(8,128)(2,1)S(1)}, bf16[128,5376]{1,0:T(8,128)(2,1)}, u32[]{:S(2)}) copy-start(bf16[128,5376]{1,0:T(8,128)(2,1)} %tokens_ref.1) | copy-start | bytes 4128772
  155.9 99.9 %copy-start.14 = (f32[5376]{0:T(1024)S(1)}, f32[5376]{0:T(1024)}, u32[]{:S(2)}) copy-start(f32[5376]{0:T(1024)} %param.10) | copy-start | bytes 64516
  255.8 2.2 copy-start.13
Sparse Core Ops, SparseCore 0:
  147.6 108.1 reduce-scatter.1

commit v3 on v2

--- a/solution.py
+++ b/solution.py
@@ -1,3 +1,5 @@
+import functools
+
 import jax
 import jax.numpy as jnp
 from jax import lax
@@ -19,10 +21,6 @@
     starts = endings - doc_lengths
     inside = starts[None, :] <= positions[:, None]
     return jnp.max(jnp.where(inside, starts[None, :], jnp.zeros_like(starts)[None, :]), axis=1)
-
-
-def input_norm(values, gain):
-    return values * lax.rsqrt(jnp.mean(values * values, axis=1, keepdims=True) + EPSILON) * gain
 
 
 def angle_tables(positions, head_size):
@@ -114,182 +112,16 @@
     return second
 
 
-def weight_sum_kernel(
-    key_ref, value_ref, key_out, value_out,
-    key_send, order, value_total, key_next, value_next, last_send, last_recv,
-    *rest,
-):
-    bufs_a, bufs_b, bufs_c, bufs_d = rest[0:6], rest[6:12], rest[12:18], rest[18:24]
-    sems = rest[24:]
-    rows = key_out.shape[0]
-    cols = key_out.shape[1]
-    big, mid = 16 * rows, 4 * rows
-    split_big = big // 2
-    split_mid = mid // 2 + mid // 2 % 16
-    place = lax.axis_index("seq")
-    member = lax.axis_index("tp")
-    x = lax.rem(place, 4)
-    z = lax.rem(place // 4, 4)
-    y = place // 16
-
-    def device(ys, zs, xs):
-        return ((ys * 4 + zs) * 4 + xs, member)
-
-    x_up, x_down = device(y, z, lax.rem(x + 1, 4)), device(y, z, lax.rem(x + 3, 4))
-    y_up, y_down = device(lax.rem(y + 1, 4), z, x), device(lax.rem(y + 3, 4), z, x)
-    z_others = [device(y, lax.rem(z + d, 4), x) for d in (1, 2, 3)]
-    barrier = pltpu.get_barrier_semaphore()
-    for other in [x_up, x_down, y_up, y_down] + z_others:
-        pl.semaphore_signal(barrier, inc=1, device_id=other, device_id_type=MESH_IDS)
-
-    pl.semaphore_wait(barrier, 7)
-
-    def finish_b1(total):
-        for part in range(4):
-            at = pl.ds(part * mid, mid)
-            value_total[at, :] = total(at)
-        for xs in range(4):
-            for zs in range(4):
-                order[zs * rows : zs * rows + rows, :] = value_total[
-                    zs * mid + xs * rows : zs * mid + xs * rows + rows, :
-                ]
-            value_next[xs] = order[...].astype(jnp.bfloat16)
-
-    second_b = ring_sum(
-        lambda t: value_ref.at[pl.ds(pl.multiple_of(t * big, 16), big)],
-        big, split_big, y, y_up, y_down, bufs_b, sems[2:4], finish_b1,
-    )
-
-    for ys in range(4):
-        for xs in range(4):
-            for zs in range(4):
-                begin = ((ys * 4 + zs) * 4 + xs) * rows
-                order[zs * rows : zs * rows + rows, :] = key_ref[begin : begin + rows, :]
-            key_send[xs, ys * mid : ys * mid + mid, :] = order[...].astype(jnp.bfloat16)
-
-    def finish_a1(total):
-        for part in range(4):
-            at = pl.ds(part * mid, mid)
-            key_next[part] = total(at).astype(jnp.bfloat16)
-
-    second_a = ring_sum(
-        lambda t: key_send.at[t],
-        big, split_big, x, x_up, x_down, bufs_a, sems[0:2], finish_a1,
-    )
-    third_b = second_b()
-    third_a = second_a()
-    drain_b = third_b()
-
-    def finish_last(at):
-        def finish(total):
-            order[...] = total(pl.ds(0, mid))
-            for zs in range(4):
-                last_send[zs, 0:rows, at : at + cols] = order[
-                    zs * rows : zs * rows + rows, :
-                ].astype(jnp.bfloat16)
-                last_send[zs, rows:, at : at + cols] = jnp.zeros(
-                    (last_send.shape[1] - rows, cols), jnp.bfloat16
-                )
-
-        return finish
-
-    second_d = ring_sum(
-        lambda t: value_next.at[t],
-        mid, split_mid, x, x_up, x_down, bufs_d, sems[6:8], finish_last(cols),
-    )
-    drain_a = third_a()
-    second_c = ring_sum(
-        lambda t: key_next.at[t],
-        mid, split_mid, y, y_up, y_down, bufs_c, sems[4:6], finish_last(0),
-    )
-    third_d = second_d()
-    third_c = second_c()
-    drain_d = third_d()
-    drain_c = third_c()
-    copies = []
-    for d in (1, 2, 3):
-        one = pltpu.make_async_remote_copy(
-            src_ref=last_send.at[lax.rem(z + d, 4)],
-            dst_ref=last_recv.at[d - 1],
-            send_sem=sems[8].at[d - 1],
-            recv_sem=sems[9].at[d - 1],
-            device_id=z_others[d - 1],
-            device_id_type=MESH_IDS,
-        )
-        one.start()
-        copies.append(one)
-    for one in copies:
-        one.wait_recv()
-    total = last_send[z, 0:rows, :].astype(jnp.float32)
-    for d in range(3):
-        total = total + last_recv[d, 0:rows, :].astype(jnp.float32)
-    key_out[...] = total[:, 0:cols]
-    value_out[...] = total[:, cols:]
-    for one in copies:
-        one.wait_send()
-    for drain in (drain_a, drain_b, drain_c, drain_d):
-        drain()
-
-
-def weight_sum(key_term, value_term):
-    depth, cols = key_term.shape
-    rows = depth // 64
-    big, mid = 16 * rows, 4 * rows
-    split_big = big // 2
-    split_mid = mid // 2 + mid // 2 % 16
-    padded = (rows + 15) // 16 * 16
-    bf = jnp.bfloat16
-
-    def bufs(size, split):
-        return [
-            pltpu.VMEM((split, cols), bf),
-            pltpu.VMEM((size - split, cols), bf),
-            pltpu.VMEM((split, cols), bf),
-            pltpu.VMEM((size - split, cols), bf),
-            pltpu.VMEM((size, cols), bf),
-            pltpu.VMEM((size, cols), bf),
-        ]
-
-    return pl.pallas_call(
-        weight_sum_kernel,
-        out_shape=[jax.ShapeDtypeStruct((rows, cols), jnp.float32)] * 2,
-        in_specs=[pl.BlockSpec(memory_space=pltpu.VMEM)] * 2,
-        out_specs=[pl.BlockSpec(memory_space=pltpu.VMEM)] * 2,
-        scratch_shapes=[
-            pltpu.VMEM((4, big, cols), bf),
-            pltpu.VMEM((mid, cols), jnp.float32),
-            pltpu.VMEM((big, cols), jnp.float32),
-            pltpu.VMEM((4, mid, cols), bf),
-            pltpu.VMEM((4, mid, cols), bf),
-            pltpu.VMEM((4, padded, 2 * cols), bf),
-            pltpu.VMEM((3, padded, 2 * cols), bf),
-        ]
-        + bufs(big, split_big)
-        + bufs(big, split_big)
-        + bufs(mid, split_mid)
-        + bufs(mid, split_mid)
-        + [pltpu.SemaphoreType.DMA((6,))] * 8
-        + [pltpu.SemaphoreType.DMA((3,))] * 2,
-        compiler_params=pltpu.CompilerParams(
-            collective_id=1, has_side_effects=True, vmem_limit_bytes=40 * 1024 * 1024
-        ),
-        cost_estimate=pl.CostEstimate(
-            flops=100_000_000, bytes_accessed=150_000_000, transcendentals=0
-        ),
-        name="weight_sum",
-    )(key_term, value_term)
-
-
 def turn(values, cosine, sine):
     return values * cosine + pltpu.roll(values, values.shape[-1] // 2, 1) * sine
 
 
 def gather_kernel(
-    tokens_ref, gain_ref, raw_ref, q_gain_ref, k_gain_ref, cos_ref, sin_ref, w_key_ref, w_value_ref,
+    tokens_hbm, gain_ref, raw_hbm, q_gain_ref, k_gain_ref, cos_ref, sin_ref, w_key_ref, w_value_ref,
     gathered_ref, query_ref, raw_key_ref, window_ref,
-    held, relay_up, relay_down, weights, window,
+    held, relay_up, relay_down, weights, window, tokens_ref, raw_ref, passing,
     weight_sem, out_sem, window_sem, relay_send, relay_recv, cross_send, cross_recv,
-    pair_send, pair_recv, chunk_send, chunk_recv, halo_send, halo_recv,
+    pair_send, pair_recv, chunk_send, chunk_recv, halo_send, halo_recv, middle_send, middle_recv,
 ):
     rows = tokens_ref.shape[0]
     half = rows // 2
@@ -311,8 +143,16 @@
 
     z_up, z_down = along_z(2), along_z(6)
     partner = (place, upper * 2 + 1 - core)
-    later = [(lax.rem(place + by, count), member) for by in (1, 2)]
-    earlier = [(lax.rem(place + count - by, count), member) for by in (1, 2)]
+    later = (lax.rem(place + 1, count), member)
+    earlier = (lax.rem(place + count - 1, count), member)
+
+    def in_row(of, xs):
+        return (of // WIDE * WIDE + xs, member)
+
+    left, right = lax.rem(x + WIDE - 1, WIDE), lax.rem(x + 1, WIDE)
+    middle_to = in_row(lax.rem(place + 2, count), left)
+    middle_from = (lax.rem(place // WIDE * WIDE + left + count - 2, count), member)
+    row_left, row_right = in_row(place, left), in_row(place, right)
 
     def remote(source, target, send_sem, recv_sem, device):
         return pltpu.make_async_remote_copy(
@@ -324,6 +164,10 @@
             device_id_type=MESH_IDS,
         )
 
+    load_tokens = pltpu.make_async_copy(tokens_hbm, tokens_ref, weight_sem.at[2])
+    load_tokens.start()
+    load_raw = pltpu.make_async_copy(raw_hbm, raw_ref, weight_sem.at[3])
+    load_raw.start()
     loads = [
         pltpu.make_async_copy(w_key_ref, weights.at[:, pl.ds(0, cols)], weight_sem.at[0]),
         pltpu.make_async_copy(w_value_ref, weights.at[:, pl.ds(cols, cols)], weight_sem.at[1]),
@@ -331,7 +175,7 @@
     for one in loads:
         one.start()
     barrier = pltpu.get_barrier_semaphore()
-    for other in [z_up, z_down, partner] + later + earlier:
+    for other in [z_up, z_down, partner, later, earlier, middle_to, middle_from, row_left, row_right]:
         pl.semaphore_signal(barrier, inc=1, device_id=other, device_id_type=MESH_IDS)
 
     own = pl.multiple_of(member * rows, rows)
@@ -348,8 +192,9 @@
         ).astype(jnp.bfloat16)
         return carry
 
+    load_tokens.wait()
     lax.fori_loop(0, rows // 16, norm_rows, 0)
-    pl.semaphore_wait(barrier, 7)
+    pl.semaphore_wait(barrier, 9)
 
     to_partner = remote(
         held.at[pl.ds(own, rows)], held.at[pl.ds(own, rows)], pair_send.at[0], pair_recv.at[0], partner
@@ -397,11 +242,22 @@
         first_down(step).start()
 
     def halo(by, index, begin, size):
+        at = pl.ds(begin, size)
         return remote(
-            window.at[2, pl.ds(begin, size)],
-            window.at[2 - by, pl.ds(begin, size)],
-            halo_send.at[by - 1, index], halo_recv.at[by - 1, index], later[by - 1],
-        )
+            window.at[2, at] if by == 1 else passing.at[at],
+            window.at[2 - by, at],
+            halo_send.at[by - 1, index], halo_recv.at[by - 1, index], later if by == 1 else row_left,
+        )
+
+    def middle(index, begin, size):
+        at = pl.ds(begin, size)
+        return remote(
+            window.at[2, at], passing.at[at], middle_send.at[index], middle_recv.at[index], middle_to
+        )
+
+    def hand_on(index, begin, size):
+        middle(index, begin, size).wait_recv()
+        halo(2, index, begin, size).start()
 
     def project(parts):
         block = [held[pl.ds(begin, size), :] for begin, size in parts]
@@ -431,7 +287,7 @@
         one.wait()
     project([(own, rows)])
     halo(1, 0, own, rows).start()
-    halo(2, 0, own, rows).start()
+    middle(0, own, rows).start()
     to_partner.wait_recv()
     out_beside = pltpu.make_async_copy(
         held.at[pl.ds(beside, rows)], gathered_ref.at[pl.ds(beside, rows)], out_sem.at[1]
@@ -439,8 +295,9 @@
     out_beside.start()
     project([(beside, rows)])
     halo(1, 1, beside, rows).start()
-    halo(2, 1, beside, rows).start()
-
+    middle(1, beside, rows).start()
+
+    load_raw.wait()
     for head in range(raw_ref.shape[1] // head_size):
         lanes = slice(head * head_size, (head + 1) * head_size)
         values = raw_ref[:, lanes].astype(jnp.float32)
@@ -455,6 +312,9 @@
         second_up(step).start()
         first_down(step).wait_recv()
         second_down(step).start()
+        if step == 1:
+            hand_on(0, own, rows)
+            hand_on(1, beside, rows)
 
     def groups(step):
         return [
@@ -472,10 +332,18 @@
         project(groups(step))
         for index, (begin, size) in enumerate(groups(step)):
             halo(1, 2 + step * 4 + index, begin, size).start()
-            halo(2, 2 + step * 4 + index, begin, size).start()
+            middle(2 + step * 4 + index, begin, size).start()
+
+        @pl.when(step > 0)
+        def before():
+            for index, (begin, size) in enumerate(groups(step - 1)):
+                hand_on(2 + (step - 1) * 4 + index, begin, size)
+
         return carry
 
     lax.fori_loop(0, 4, arrive, 0)
+    for index, (begin, size) in enumerate(groups(3)):
+        hand_on(14 + index, begin, size)
     out_across = pltpu.make_async_copy(
         held.at[pl.ds(across, rows)], gathered_ref.at[pl.ds(across, rows)], out_sem.at[2]
     )
@@ -485,22 +353,23 @@
     out_across.start()
     out_corner.start()
 
-    def each_halo(act):
-        for by in (1, 2):
-            act(halo(by, 0, own, rows))
-            act(halo(by, 1, beside, rows))
+    def each_halo(kinds, act):
+        for kind in kinds:
+            act(kind(0, own, rows))
+            act(kind(1, beside, rows))
 
             def inner(step, carry):
                 for index, (begin, size) in enumerate(groups(step)):
-                    act(halo(by, 2 + step * 4 + index, begin, size))
+                    act(kind(2 + step * 4 + index, begin, size))
                 return carry
 
             lax.fori_loop(0, 4, inner, 0)
 
-    each_halo(lambda copy: copy.wait_recv())
+    halos = [functools.partial(halo, 1), functools.partial(halo, 2)]
+    each_halo(halos, lambda copy: copy.wait_recv())
     out_window = pltpu.make_async_copy(window, window_ref, window_sem.at[0])
     out_window.start()
-    each_halo(lambda copy: copy.wait_send())
+    each_halo(halos + [middle], lambda copy: copy.wait_send())
     to_partner.wait_send()
     for step in range(4):
         first_up(step).wait_send()
@@ -520,6 +389,7 @@
     bf = jnp.bfloat16
     vmem = pl.BlockSpec(memory_space=pltpu.VMEM)
     anywhere = pl.BlockSpec(memory_space=pl.ANY)
+    outside = pl.BlockSpec(memory_space=pltpu.HBM)
     dma = pltpu.SemaphoreType.DMA
     return pl.pallas_call(
         gather_kernel,
@@ -529,7 +399,7 @@
             jax.ShapeDtypeStruct((shard, cols), jnp.float32),
             jax.ShapeDtypeStruct((3, shard, 2 * cols), bf),
         ],
-        in_specs=[vmem] * 7 + [anywhere] * 2,
+        in_specs=[outside, vmem, outside] + [vmem] * 4 + [outside] * 2,
         out_specs=[anywhere, vmem, vmem, anywhere],
         scratch_shapes=[
             pltpu.VMEM((shard, depth), bf),
@@ -537,7 +407,10 @@
             pltpu.VMEM((rows // 2, depth), bf),
             pltpu.VMEM((depth, 2 * cols), bf),
             pltpu.VMEM((3, shard, 2 * cols), bf),
-            dma((2,)),
+            pltpu.VMEM((rows, depth), bf),
+            pltpu.VMEM(raw_queries.shape, bf),
+            pltpu.VMEM((shard, 2 * cols), bf),
+            dma((4,)),
             dma((4,)),
             dma((1,)),
             dma((2, 4)),
@@ -550,9 +423,11 @@
             dma((2, 4)),
             dma((2, 18)),
             dma((2, 18)),
+            dma((18,)),
+            dma((18,)),
         ],
         compiler_params=pltpu.CompilerParams(
-            collective_id=2, has_side_effects=True, vmem_limit_bytes=40 * 1024 * 1024
+            collective_id=2, has_side_effects=True, vmem_limit_bytes=60 * 1024 * 1024
         ),
         cost_estimate=pl.CostEstimate(
             flops=3_000_000_000, bytes_accessed=150_000_000, transcendentals=0
@@ -573,10 +448,10 @@
 
 
 def attend_kernel(
-    query_ref, window_ref, out_grad_ref, low_ref, raw_ref, raw_key_ref, cos_ref, sin_ref, q_gain_ref, k_gain_ref,
+    query_ref, window_ref, out_grad_hbm, low_ref, raw_hbm, raw_key_ref, cos_ref, sin_ref, q_gain_ref, k_gain_ref,
     grad_query_ref, grad_kv_ref,
-    exps, along, totals, query_total, parts, returned,
-    send_sem, recv_sem,
+    exps, along, totals, query_total, parts, returned, out_grad_ref, raw_ref, passing,
+    send_sem, recv_sem, middle_send, middle_recv, load_sem,
 ):
     shard = query_ref.shape[0]
     head_size = q_gain_ref.shape[1]
@@ -587,10 +462,23 @@
     place = lax.axis_index("seq")
     member = lax.axis_index("tp")
     count = lax.axis_size("seq")
-    later = [(lax.rem(place + by, count), member) for by in (2, 1)]
-    earlier = [(lax.rem(place + count - by, count), member) for by in (2, 1)]
+    x = lax.rem(place, WIDE)
+
+    def in_row(of, xs):
+        return (of // WIDE * WIDE + xs, member)
+
+    left, right = lax.rem(x + WIDE - 1, WIDE), lax.rem(x + 1, WIDE)
+    later = (lax.rem(place + 1, count), member)
+    earlier = (lax.rem(place + count - 1, count), member)
+    middle_to = in_row(lax.rem(place + count - 2, count), right)
+    middle_from = (lax.rem(place // WIDE * WIDE + right + 2, count), member)
+    row_left, row_right = in_row(place, left), in_row(place, right)
+    load_grads = pltpu.make_async_copy(out_grad_hbm, out_grad_ref, load_sem.at[0])
+    load_grads.start()
+    load_raw = pltpu.make_async_copy(raw_hbm, raw_ref, load_sem.at[1])
+    load_raw.start()
     barrier = pltpu.get_barrier_semaphore()
-    for other in later + earlier:
+    for other in [later, earlier, middle_to, middle_from, row_left, row_right]:
         pl.semaphore_signal(barrier, inc=1, device_id=other, device_id_type=MESH_IDS)
 
     totals[...] = jnp.zeros_like(totals)
@@ -600,14 +488,26 @@
 
     def back(window, head):
         return pltpu.make_async_remote_copy(
-            src_ref=parts.at[window, head],
+            src_ref=parts.at[window, head] if window == 1 else passing.at[head],
             dst_ref=returned.at[window, head],
             send_sem=send_sem.at[window, head],
             recv_sem=recv_sem.at[window, head],
-            device_id=earlier[window],
+            device_id=earlier if window == 1 else row_right,
             device_id_type=MESH_IDS,
         )
 
+    def middle(head):
+        return pltpu.make_async_remote_copy(
+            src_ref=parts.at[0, head],
+            dst_ref=passing.at[head],
+            send_sem=middle_send.at[head],
+            recv_sem=middle_recv.at[head],
+            device_id=middle_to,
+            device_id_type=MESH_IDS,
+        )
+
+    load_grads.wait()
+    load_raw.wait()
     for head in range(kv_heads):
         key_lanes = slice(head * head_size, (head + 1) * head_size)
         value_lanes = slice((kv_heads + head) * head_size, (kv_heads + head + 1) * head_size)
@@ -675,10 +575,13 @@
             parts[window, head, :, :head_size] = totals[rows, key_lanes].astype(jnp.bfloat16)
             parts[window, head, :, head_size:] = totals[rows, value_lanes].astype(jnp.bfloat16)
         if head == 0:
-            pl.semaphore_wait(barrier, 4)
-        for window in range(2):
-            back(window, head).start()
-
+            pl.semaphore_wait(barrier, 6)
+        middle(head).start()
+        back(1, head).start()
+
+    for head in range(kv_heads):
+        middle(head).wait_recv()
+        back(0, head).start()
     own = slice(reach, reach + shard)
     for head in range(kv_heads):
         key_lanes = slice(head * head_size, (head + 1) * head_size)
@@ -696,6 +599,7 @@
             jnp.bfloat16
         )
     for head in range(kv_heads):
+        middle(head).wait_send()
         for window in range(2):
             back(window, head).wait_send()
 
@@ -708,13 +612,14 @@
     tile = shard // 2
     width = group_size * tile
     vmem = pl.BlockSpec(memory_space=pltpu.VMEM)
+    outside = pl.BlockSpec(memory_space=pltpu.HBM)
     return pl.pallas_call(
         attend_kernel,
         out_shape=[
             jax.ShapeDtypeStruct(query_rot.shape, jnp.bfloat16),
             jax.ShapeDtypeStruct((shard, 2 * raw_keys.shape[1]), jnp.bfloat16),
         ],
-        in_specs=[vmem] * 10,
+        in_specs=[vmem, vmem, outside, vmem, outside] + [vmem] * 5,
         out_specs=[vmem] * 2,
         scratch_shapes=[
             pltpu.VMEM((2 * shard + tile, width), jnp.float32),
@@ -723,11 +628,17 @@
             pltpu.VMEM((head_size, width), jnp.float32),
             pltpu.VMEM((2, kv_heads, shard, 2 * head_size), jnp.bfloat16),
             pltpu.VMEM((2, kv_heads, shard, 2 * head_size), jnp.bfloat16),
+            pltpu.VMEM(query_rot.shape, jnp.bfloat16),
+            pltpu.VMEM(query_rot.shape, jnp.bfloat16),
+            pltpu.VMEM((kv_heads, shard, 2 * head_size), jnp.bfloat16),
             pltpu.SemaphoreType.DMA((2, kv_heads)),
             pltpu.SemaphoreType.DMA((2, kv_heads)),
+            pltpu.SemaphoreType.DMA((kv_heads,)),
+            pltpu.SemaphoreType.DMA((kv_heads,)),
+            pltpu.SemaphoreType.DMA((2,)),
         ],
         compiler_params=pltpu.CompilerParams(
-            collective_id=3, has_side_effects=True, vmem_limit_bytes=40 * 1024 * 1024
+            collective_id=3, has_side_effects=True, vmem_limit_bytes=60 * 1024 * 1024
         ),
         cost_estimate=pl.CostEstimate(
             flops=8_000_000_000, bytes_accessed=100_000_000, transcendentals=3_000_000
@@ -739,11 +650,345 @@
     )
 
 
+def finish_kernel(
+    gathered_ref, grad_ref, w_key_ref, w_value_ref, tokens_ref, gain_ref,
+    key_out, value_out, grad_x_ref,
+    held, weights, tokens, total_own, corner_out, corner_in, beside_out, beside_in, cross_out, cross_in,
+    relay_up, relay_down,
+    key_term, value_term, key_send, order, value_total, key_next, value_next, last_send, last_recv,
+    *rest,
+):
+    bufs_a, bufs_b, bufs_c, bufs_d = rest[0:6], rest[6:12], rest[12:18], rest[18:24]
+    sems = rest[24:34]
+    load_sem, weight_sem, pair_send, pair_recv, relay_send, relay_recv, cross_send, cross_recv = rest[34:]
+    depth = gain_ref.shape[1]
+    block = tokens_ref.shape[0]
+    rows = key_out.shape[0]
+    cols = key_out.shape[1]
+    half = block // 2
+    piece = half // 4
+    big, mid = 16 * rows, 4 * rows
+    split_big = big // 2
+    split_mid = mid // 2 + mid // 2 % 16
+    slab = 768 if depth % 768 == 0 else 128
+    strip = 384 if depth % 384 == 0 else 128
+    place = lax.axis_index("seq")
+    member = lax.axis_index("tp")
+    core = lax.rem(member, 2)
+    upper = member // 2
+    x = lax.rem(place, 4)
+    z = lax.rem(place // 4, 4)
+    y = place // 16
+    height = upper * 4 + z
+
+    def device(ys, zs, xs):
+        return ((ys * 4 + zs) * 4 + xs, member)
+
+    def along_z(by):
+        other = lax.rem(height + by, 8)
+        return ((y * 4 + lax.rem(other, 4)) * 4 + x, other // 4 * 2 + core)
+
+    def remote(source, target, send_sem, recv_sem, to):
+        return pltpu.make_async_remote_copy(
+            src_ref=source,
+            dst_ref=target,
+            send_sem=send_sem,
+            recv_sem=recv_sem,
+            device_id=to,
+            device_id_type=MESH_IDS,
+        )
+
+    def weight_load(step):
+        at = pl.ds(pl.multiple_of(step * slab, slab), slab)
+        return (
+            pltpu.make_async_copy(w_key_ref.at[at], weights.at[at, pl.ds(0, cols)], weight_sem.at[0, step]),
+            pltpu.make_async_copy(w_value_ref.at[at], weights.at[at, pl.ds(cols, cols)], weight_sem.at[1, step]),
+        )
+
+    for step in range(depth // slab):
+        for one in weight_load(step):
+            one.start()
+    load_held = pltpu.make_async_copy(gathered_ref, held, load_sem.at[0])
+    load_held.start()
+    load_tokens = pltpu.make_async_copy(tokens_ref, tokens, load_sem.at[1])
+    load_tokens.start()
+
+    z_up, z_down = along_z(2), along_z(6)
+    partner = (place, upper * 2 + 1 - core)
+    x_up, x_down = device(y, z, lax.rem(x + 1, 4)), device(y, z, lax.rem(x + 3, 4))
+    y_up, y_down = device(lax.rem(y + 1, 4), z, x), device(lax.rem(y + 3, 4), z, x)
+    z_others = [device(y, lax.rem(z + d, 4), x) for d in (1, 2, 3)]
+    barrier = pltpu.get_barrier_semaphore()
+    for other in [z_up, z_down, partner, x_up, x_down, y_up, y_down] + z_others:
+        pl.semaphore_signal(barrier, inc=1, device_id=other, device_id_type=MESH_IDS)
+
+    own = pl.multiple_of(member * block, block)
+    beside = pl.multiple_of((upper * 2 + 1 - core) * block, block)
+    across = pl.multiple_of(((1 - upper) * 2 + core) * block, block)
+    corner = pl.multiple_of(((1 - upper) * 2 + 1 - core) * block, block)
+
+    def part(begin, store, first=False):
+        grads = grad_ref[pl.ds(begin, block), :]
+
+        def one_slab(step, carry):
+            if first:
+                for one in weight_load(step):
+                    one.wait()
+            at = pl.ds(pl.multiple_of(step * slab, slab), slab)
+            store(at, contract_last(grads, weights[at, :]))
+            return carry
+
+        lax.fori_loop(0, depth // slab, one_slab, 0)
+
+    def store_corner(at, value):
+        corner_out[:, at] = value.astype(jnp.bfloat16)
+
+    part(corner, store_corner, first=True)
+    pl.semaphore_wait(barrier, 10)
+    send_corner = remote(corner_out, corner_in, pair_send.at[0], pair_recv.at[0], partner)
+    send_corner.start()
+
+    def store_total(at, value):
+        total_own[:, at] = value
+
+    part(across, store_total)
+    send_corner.wait_recv()
+
+    def join(step, carry):
+        at = pl.ds(pl.multiple_of(step * 16, 16), 16)
+        cross_out[at, :] = (total_own[at, :] + corner_in[at, :].astype(jnp.float32)).astype(jnp.bfloat16)
+        return carry
+
+    lax.fori_loop(0, block // 16, join, 0)
+
+    def rows_at(side, step):
+        return pl.ds(side * half + step * piece, piece)
+
+    def small(step):
+        return pl.ds(step * piece, piece)
+
+    first = [
+        [
+            remote(cross_out.at[rows_at(0, step)], relay_up.at[small(step)], relay_send.at[0, step], relay_recv.at[0, step], z_up),
+            remote(cross_out.at[rows_at(1, step)], relay_down.at[small(step)], relay_send.at[1, step], relay_recv.at[1, step], z_down),
+        ]
+        for step in range(4)
+    ]
+    second = [
+        [
+            remote(relay_up.at[small(step)], cross_in.at[rows_at(0, step)], cross_send.at[0, step], cross_recv.at[0, step], z_up),
+            remote(relay_down.at[small(step)], cross_in.at[rows_at(1, step)], cross_send.at[1, step], cross_recv.at[1, step], z_down),
+        ]
+        for step in range(4)
+    ]
+    for pair in first:
+        for one in pair:
+            one.start()
+
+    def relay(step):
+        for side in (0, 1):
+            first[step][side].wait_recv()
+            second[step][side].start()
+
+    load_held.wait()
+
+    def strips(step, carry):
+        at = pl.ds(pl.multiple_of(step * strip, strip), strip)
+        result = contract_first(held[:, at], grad_ref[...])
+        key_term[at, :] = result[:, :cols]
+        value_term[at, :] = result[:, cols:].astype(jnp.bfloat16)
+        return carry
+
+    lax.fori_loop(0, depth // strip, strips, 0)
+
+    def finish_b1(total):
+        for quarter in range(4):
+            at = pl.ds(quarter * mid, mid)
+            value_total[at, :] = total(at)
+        for xs in range(4):
+            for zs in range(4):
+                order[zs * rows : zs * rows + rows, :] = value_total[
+                    zs * mid + xs * rows : zs * mid + xs * rows + rows, :
+                ]
+            value_next[xs] = order[...].astype(jnp.bfloat16)
+
+    second_b = ring_sum(
+        lambda t: value_term.at[pl.ds(pl.multiple_of(t * big, 16), big)],
+        big, split_big, y, y_up, y_down, bufs_b, sems[2:4], finish_b1,
+    )
+
+    for ys in range(4):
+        for xs in range(4):
+            for zs in range(4):
+                begin = ((ys * 4 + zs) * 4 + xs) * rows
+                order[zs * rows : zs * rows + rows, :] = key_term[begin : begin + rows, :]
+            key_send[xs, ys * mid : ys * mid + mid, :] = order[...].astype(jnp.bfloat16)
+
+    def finish_a1(total):
+        for quarter in range(4):
+            at = pl.ds(quarter * mid, mid)
+            key_next[quarter] = total(at).astype(jnp.bfloat16)
+
+    second_a = ring_sum(
+        lambda t: key_send.at[t],
+        big, split_big, x, x_up, x_down, bufs_a, sems[0:2], finish_a1,
+    )
+    relay(0)
+
+    def store_beside(at, value):
+        beside_out[:, at] = value.astype(jnp.bfloat16)
+
+    part(beside, store_beside)
+    send_beside = remote(beside_out, beside_in, pair_send.at[1], pair_recv.at[1], partner)
+    send_beside.start()
+    part(own, store_total)
+    relay(1)
+    third_b = second_b()
+    third_a = second_a()
+    relay(2)
+    drain_b = third_b()
+
+    def finish_last(at):
+        def finish(total):
+            order[...] = total(pl.ds(0, mid))
+            for zs in range(4):
+                last_send[zs, 0:rows, at : at + cols] = order[
+                    zs * rows : zs * rows + rows, :
+                ].astype(jnp.bfloat16)
+                last_send[zs, rows:, at : at + cols] = jnp.zeros(
+                    (last_send.shape[1] - rows, cols), jnp.bfloat16
+                )
+
+        return finish
+
+    second_d = ring_sum(
+        lambda t: value_next.at[t],
+        mid, split_mid, x, x_up, x_down, bufs_d, sems[6:8], finish_last(cols),
+    )
+    relay(3)
+    drain_a = third_a()
+    second_c = ring_sum(
+        lambda t: key_next.at[t],
+        mid, split_mid, y, y_up, y_down, bufs_c, sems[4:6], finish_last(0),
+    )
+    third_d = second_d()
+    third_c = second_c()
+    drain_d = third_d()
+    drain_c = third_c()
+    copies = []
+    for d in (1, 2, 3):
+        one = remote(
+            last_send.at[lax.rem(z + d, 4)], last_recv.at[d - 1], sems[8].at[d - 1], sems[9].at[d - 1], z_others[d - 1]
+        )
+        one.start()
+        copies.append(one)
+
+    load_tokens.wait()
+    send_beside.wait_recv()
+    for step in range(4):
+        for side in (0, 1):
+            second[step][side].wait_recv()
+            at = rows_at(side, step)
+            grad = (
+                total_own[at, :] + beside_in[at, :].astype(jnp.float32) + cross_in[at, :].astype(jnp.float32)
+            )
+            grad_x_ref[at, :] = norm_back(grad, tokens[at, :].astype(jnp.float32), gain_ref[...]).astype(
+                jnp.bfloat16
+            )
+
+    for one in copies:
+        one.wait_recv()
+    total = last_send[z, 0:rows, :].astype(jnp.float32)
+    for d in range(3):
+        total = total + last_recv[d, 0:rows, :].astype(jnp.float32)
+    key_out[...] = total[:, 0:cols]
+    value_out[...] = total[:, cols:]
+    for one in copies:
+        one.wait_send()
+    for drain in (drain_a, drain_b, drain_c, drain_d):
+        drain()
+    send_corner.wait_send()
+    send_beside.wait_send()
+    for pair in first + second:
+        for one in pair:
+            one.wait_send()
+
+
+def finish(gathered, grad_kv, w_key, w_value, tokens, in_gain):
+    shard, depth = gathered.shape
+    block = tokens.shape[0]
+    cols = w_key.shape[1]
+    rows = depth // 64
+    big, mid = 16 * rows, 4 * rows
+    split_big = big // 2
+    split_mid = mid // 2 + mid // 2 % 16
+    padded = (rows + 15) // 16 * 16
+    slabs = depth // (768 if depth % 768 == 0 else 128)
+    bf = jnp.bfloat16
+    dma = pltpu.SemaphoreType.DMA
+    vmem = pl.BlockSpec(memory_space=pltpu.VMEM)
+    outside = pl.BlockSpec(memory_space=pltpu.HBM)
+
+    def bufs(size, split):
+        return [
+            pltpu.VMEM((split, cols), bf),
+            pltpu.VMEM((size - split, cols), bf),
+            pltpu.VMEM((split, cols), bf),
+            pltpu.VMEM((size - split, cols), bf),
+            pltpu.VMEM((size, cols), bf),
+            pltpu.VMEM((size, cols), bf),
+        ]
+
+    return pl.pallas_call(
+        finish_kernel,
+        out_shape=[
+            jax.ShapeDtypeStruct((rows, cols), jnp.float32),
+            jax.ShapeDtypeStruct((rows, cols), jnp.float32),
+            jax.ShapeDtypeStruct((block, depth), bf),
+        ],
+        in_specs=[outside, vmem, outside, outside, outside, vmem],
+        out_specs=[vmem] * 3,
+        scratch_shapes=[
+            pltpu.VMEM((shard, depth), bf),
+            pltpu.VMEM((depth, 2 * cols), bf),
+            pltpu.VMEM((block, depth), bf),
+            pltpu.VMEM((block, depth), jnp.float32),
+        ]
+        + [pltpu.VMEM((block, depth), bf)] * 6
+        + [pltpu.VMEM((block // 2, depth), bf)] * 2
+        + [
+            pltpu.VMEM((depth, cols), jnp.float32),
+            pltpu.VMEM((depth, cols), bf),
+            pltpu.VMEM((4, big, cols), bf),
+            pltpu.VMEM((mid, cols), jnp.float32),
+            pltpu.VMEM((big, cols), jnp.float32),
+            pltpu.VMEM((4, mid, cols), bf),
+            pltpu.VMEM((4, mid, cols), bf),
+            pltpu.VMEM((4, padded, 2 * cols), bf),
+            pltpu.VMEM((3, padded, 2 * cols), bf),
+        ]
+        + bufs(big, split_big)
+        + bufs(big, split_big)
+        + bufs(mid, split_mid)
+        + bufs(mid, split_mid)
+        + [dma((6,))] * 8
+        + [dma((3,))] * 2
+        + [dma((2,)), dma((2, slabs)), dma((2,)), dma((2,))]
+        + [dma((2, 4))] * 4,
+        compiler_params=pltpu.CompilerParams(
+            collective_id=1, has_side_effects=True, vmem_limit_bytes=60 * 1024 * 1024
+        ),
+        cost_estimate=pl.CostEstimate(
+            flops=6_000_000_000, bytes_accessed=150_000_000, transcendentals=0
+        ),
+        name="finish",
+    )(gathered, grad_kv, w_key, w_value, tokens, in_gain[None, :])
+
+
 def shards(tokens, in_gain, raw_queries, w_key, w_value, q_gain, k_gain, doc_lengths, out_grad):
     head_size = q_gain.shape[0]
     shard_rows = tokens.shape[0] * lax.axis_size("tp")
     reach = 2 * shard_rows
-    x_float = tokens.astype(jnp.float32)
     first_row = lax.axis_index("seq") * shard_rows
     positions = first_row + jnp.arange(shard_rows, dtype=jnp.int32)
     begins = doc_begin(doc_lengths, positions)
@@ -756,22 +1001,7 @@
     grad_queries, grad_kv = attend_back(
         query_rot, window, out_grad, low, raw_queries, raw_keys, cosine, sine, q_gain, k_gain
     )
-    kv_cols = w_key.shape[1]
-    grad_k = grad_kv[:, :kv_cols]
-    grad_v = grad_kv[:, kv_cols:]
-    partial_sum = contract_last(grad_k, w_key) + contract_last(grad_v, w_value)
-    normed_grad = lax.psum_scatter(
-        partial_sum.astype(jnp.bfloat16), "tp", scatter_dimension=0, tiled=True
-    ).astype(jnp.float32)
-
-    def norm_map(values):
-        return input_norm(values, in_gain)
-
-    unused_rows, input_back = jax.vjp(norm_map, x_float)
-    grad_x = input_back(normed_grad)[0].astype(jnp.bfloat16)
-    key_term = contract_first(gathered, grad_k)
-    value_term = contract_first(gathered, grad_v).astype(jnp.bfloat16)
-    grad_wk, grad_wv = weight_sum(key_term, value_term)
+    grad_wk, grad_wv, grad_x = finish(gathered, grad_kv, w_key, w_value, tokens, in_gain)
     return (grad_x, grad_queries, grad_wk, grad_wv)
 
 

time: 271 us -> 234 us (0.86)
  matrix products: 14.3 us -> 0 us
  between operations: 14.2 us -> 0.71 us
  local copies, waits for them, and re-layouts: 11 us -> 6.75 us
    pallas_call x1, Pallas kernels: 81.3 us -> 95.6 us  [gather_and_project(): pl.pallas_call(gather_kernel, out_shape=[jax.ShapeDtypeStruct((shard, dep...]
    dot_general x4 -> x0, matrix products: 14.3 us -> none  [the longest x2 8.41 us: contract_first(): lax.dot_general(left, right, (((0,), (0,)), ((), ())), preferred_element_...]
    pallas_call x1, Pallas kernels: 98 us -> 86.2 us  [finish(): pl.pallas_call(finish_kernel, out_shape=[jax.ShapeDtypeStruct((rows, cols...]
    unnamed x33 -> x10, local copies, waits for them, and re-layouts: 9.49 us -> 4.65 us
  transfers between devices with their start and end apart: 1 -> 0, of which waited for: 1 -> 0; matrix products, arithmetic and copies ran while one was open for 3% -> 0% of each run, Pallas kernels for 36% -> 0%
where the time goes in v3:
time: 234 us; the launch traced here: 232 us
  Pallas kernels  221 us (94%)
  local copies, waits for them, and re-layouts  6.75 us (3%)
  other arithmetic  3.52 us (2%)
    pallas_call x1, Pallas kernels, gather_and_project(): pl.pallas_call(gather_kernel, out_shape=[jax.ShapeDtypeStruct((shard, dep...  95.6 us
    pallas_call x1, Pallas kernels, finish(): pl.pallas_call(finish_kernel, out_shape=[jax.ShapeDtypeStruct((rows, cols...  86.2 us
    pallas_call x1, Pallas kernels, attend_back(): pl.pallas_call(attend_kernel, out_shape=[jax.ShapeDtypeStruct(query_rot.s...  39.5 us

profile of v3, /device:TPU:61, one launch (start us, length us, event | category | flops | bytes accessed | tf_op | source)
XLA Modules:
  0.0 232.3 jit_solution(472995413993748055)
XLA Ops:
  0.7 0.7 copy.15
  1.4 0.1 reduce-window.9
  1.5 0.1 reduce
  1.6 0.7 sub.30
  2.2 0.1 select_reduce_fusion
  2.3 0.6 maximum_subtract_fusion.low_ref
  2.9 1.4 broadcast_in_dim.20.gain_ref
  4.3 1.0 fusion
  5.3 1.0 pad_maximum_fusion
  6.3 95.6 %gather_and_project.1 = (bf16[512,5376]{1,0:T(8,128)(2,1)}, bf16[512,512]{1,0:T(8,128)(2,1)}, f32[512,256]{1,0:T(8,128)}, bf16[3,512,512]{2,1,0:T(8,128)(2,1)}) custom-call(bf16[128,5376]{1,0:T(8,128)(2,1)} %tokens_ref.1, f32[1,5376]{1,0:T(1,128)} %broadcast_in_dim.20.gain_ref, bf16[512,512]{1,0:T(8,128)(2,1)} %raw_hbm.3, f32[1,128]{1,0:T(1,128)} %bitcast.7, ...), custom_call_target="tpu_custom_call" | custom-call | flops 3000000000 | bytes 150000000 | tf_op jit(solution)/shard_map/gather_and_project/pallas_call | solution.py:394
  101.9 39.5 %attend_back.1 = (bf16[512,512]{1,0:T(8,128)(2,1)}, bf16[512,512]{1,0:T(8,128)(2,1)}) custom-call(bf16[512,512]{1,0:T(8,128)(2,1)} %get-tuple-element.14.query_ref, bf16[1536,512]{1,0:T(8,128)(2,1)} %bitcast.11, bf16[512,512]{1,0:T(8,128)(2,1)} %out_grad_hbm.1, s32[2,1,256]{2,1,0:T(1,128)} %maximum_subtract_fusion.low_ref, bf16[512,512]{1,0:T(8,128)(2,1)} %raw_hbm.3, ...), custom_call_target="tpu_custom_call" | custom-call | flops 8000000000 | bytes 100000000 | tf_op jit(solution)/shard_map/attend_back/pallas_call | solution.py:616
  141.5 86.2 %finish.1 = (f32[84,256]{1,0:T(8,128)}, f32[84,256]{1,0:T(8,128)}, bf16[128,5376]{1,0:T(8,128)(2,1)}) custom-call(bf16[512,5376]{1,0:T(8,128)(2,1)} %get-tuple-element.13.gathered_ref, bf16[512,512]{1,0:T(8,128)(2,1)} %get-tuple-element.17.grad_ref, bf16[5376,256]{1,0:T(8,128)(2,1)} %w_key_ref.3, bf16[5376,256]{1,0:T(8,128)(2,1)} %w_value_ref.3, ...), custom_call_target="tpu_custom_call" | custom-call | flops 6000000000 | bytes 150000000 | tf_op jit(solution)/shard_map/finish/pallas_call | solution.py:942
  227.6 0.0 copy-start
  227.7 0.0 copy-start.2
  227.7 0.0 copy-start.1
  227.7 2.6 %copy.20 = bf16[128,5376]{1,0:T(8,128)(2,1)} copy(bf16[128,5376]{1,0:T(8,128)(2,1)} %get-tuple-element.31) | data formatting | bytes 2752512
  230.2 0.0 copy-done
  230.2 0.8 copy.21
  231.0 0.0 copy-done.2
  231.0 0.6 copy.22
  231.7 0.0 copy-done.1
  231.7 0.6 copy.23
  (3 shorter events, 0.0 us)
Async XLA Ops:
  227.6 2.6 %copy-start = (bf16[512,512]{1,0:T(8,128)(2,1)S(1)}, bf16[512,512]{1,0:T(8,128)(2,1)}, u32[]{:S(2)}) copy-start(bf16[512,512]{1,0:T(8,128)(2,1)} %get-tuple-element.32) | copy-start | bytes 1572868
  227.7 3.4 %copy-start.2 = (f32[84,256]{1,0:T(8,128)S(1)}, f32[84,256]{1,0:T(8,128)}, u32[]{:S(2)}) copy-start(f32[84,256]{1,0:T(8,128)} %get-tuple-element.33) | copy-start | bytes 258052
  227.7 4.0 %copy-start.1 = (f32[84,256]{1,0:T(8,128)S(1)}, f32[84,256]{1,0:T(8,128)}, u32[]{:S(2)}) copy-start(f32[84,256]{1,0:T(8,128)} %get-tuple-element.34) | copy-start | bytes 258052

commit v4 on v3

--- a/solution.py
+++ b/solution.py
@@ -150,9 +150,9 @@
         return (of // WIDE * WIDE + xs, member)
 
     left, right = lax.rem(x + WIDE - 1, WIDE), lax.rem(x + 1, WIDE)
-    middle_to = in_row(lax.rem(place + 2, count), left)
-    middle_from = (lax.rem(place // WIDE * WIDE + left + count - 2, count), member)
     row_left, row_right = in_row(place, left), in_row(place, right)
+    second_to = (lax.rem(place // WIDE * WIDE + right + 2, count), member)
+    second_from = in_row(lax.rem(place + count - 2, count), lax.rem(x + 2 * WIDE - 3, WIDE))
 
     def remote(source, target, send_sem, recv_sem, device):
         return pltpu.make_async_remote_copy(
@@ -175,7 +175,7 @@
     for one in loads:
         one.start()
     barrier = pltpu.get_barrier_semaphore()
-    for other in [z_up, z_down, partner, later, earlier, middle_to, middle_from, row_left, row_right]:
+    for other in [z_up, z_down, partner, later, earlier, second_to, second_from, row_left, row_right]:
         pl.semaphore_signal(barrier, inc=1, device_id=other, device_id_type=MESH_IDS)
 
     own = pl.multiple_of(member * rows, rows)
@@ -237,7 +237,7 @@
         at = pl.ds(pl.multiple_of(across + side * half + step * piece, piece), piece)
         return remote(held.at[at], held.at[at], chunk_send.at[side, step], chunk_recv.at[side, step], partner)
 
-    for step in range(4):
+    for step in range(2):
         first_up(step).start()
         first_down(step).start()
 
@@ -246,13 +246,13 @@
         return remote(
             window.at[2, at] if by == 1 else passing.at[at],
             window.at[2 - by, at],
-            halo_send.at[by - 1, index], halo_recv.at[by - 1, index], later if by == 1 else row_left,
+            halo_send.at[by - 1, index], halo_recv.at[by - 1, index], later if by == 1 else second_to,
         )
 
     def middle(index, begin, size):
         at = pl.ds(begin, size)
         return remote(
-            window.at[2, at], passing.at[at], middle_send.at[index], middle_recv.at[index], middle_to
+            window.at[2, at], passing.at[at], middle_send.at[index], middle_recv.at[index], row_left
         )
 
     def hand_on(index, begin, size):
@@ -296,6 +296,9 @@
     project([(beside, rows)])
     halo(1, 1, beside, rows).start()
     middle(1, beside, rows).start()
+    for step in range(2, 4):
+        first_up(step).start()
+        first_down(step).start()
 
     load_raw.wait()
     for head in range(raw_ref.shape[1] // head_size):
@@ -312,7 +315,7 @@
         second_up(step).start()
         first_down(step).wait_recv()
         second_down(step).start()
-        if step == 1:
+        if step == 0:
             hand_on(0, own, rows)
             hand_on(1, beside, rows)
 
@@ -327,18 +330,18 @@
         for side, copy in ((0, second_up(step)), (1, second_down(step))):
             copy.wait_recv()
             pass_on(side, step).start()
+
+        @pl.when(step > 0)
+        def before():
+            for index, (begin, size) in enumerate(groups(step - 1)):
+                hand_on(2 + (step - 1) * 4 + index, begin, size)
+
         for side in (0, 1):
             pass_on(side, step).wait_recv()
         project(groups(step))
         for index, (begin, size) in enumerate(groups(step)):
             halo(1, 2 + step * 4 + index, begin, size).start()
             middle(2 + step * 4 + index, begin, size).start()
-
-        @pl.when(step > 0)
-        def before():
-            for index, (begin, size) in enumerate(groups(step - 1)):
-                hand_on(2 + (step - 1) * 4 + index, begin, size)
-
         return carry
 
     lax.fori_loop(0, 4, arrive, 0)
@@ -976,7 +979,7 @@
         + [dma((2,)), dma((2, slabs)), dma((2,)), dma((2,))]
         + [dma((2, 4))] * 4,
         compiler_params=pltpu.CompilerParams(
-            collective_id=1, has_side_effects=True, vmem_limit_bytes=60 * 1024 * 1024
+            collective_id=1, has_side_effects=True, vmem_limit_bytes=51 * 1024 * 1024
         ),
         cost_estimate=pl.CostEstimate(
             flops=6_000_000_000, bytes_accessed=150_000_000, transcendentals=0

time: 234 us -> 223 us (0.953)
  Pallas kernels: 221 us -> 208 us
    pallas_call x1, Pallas kernels: 95.6 us -> 88 us  [gather_and_project(): pl.pallas_call(gather_kernel, out_shape=[jax.ShapeDtypeStruct((shard, dep...]
    pallas_call x1, Pallas kernels: 86.2 us -> 82.3 us  [finish(): pl.pallas_call(finish_kernel, out_shape=[jax.ShapeDtypeStruct((rows, cols...]
where the time goes in v4:
time: 223 us; the launch traced here: 219 us
  Pallas kernels  208 us (93%)
  local copies, waits for them, and re-layouts  6.57 us (3%)
  other arithmetic  3.52 us (2%)
    pallas_call x1, Pallas kernels, gather_and_project(): pl.pallas_call(gather_kernel, out_shape=[jax.ShapeDtypeStruct((shard, dep...  88 us
    pallas_call x1, Pallas kernels, finish(): pl.pallas_call(finish_kernel, out_shape=[jax.ShapeDtypeStruct((rows, cols...  82.3 us
    pallas_call x1, Pallas kernels, attend_back(): pl.pallas_call(attend_kernel, out_shape=[jax.ShapeDtypeStruct(query_rot.s...  37.9 us
    unnamed x10, local copies, waits for them, and re-layouts  4.47 us

profile of v4, /device:TPU:61, one launch (start us, length us, event | category | flops | bytes accessed | tf_op | source)
XLA Modules:
  0.0 219.1 jit_solution(5080891322038389067)
XLA Ops:
  0.7 0.7 copy.15
  1.4 0.1 reduce-window.9
  1.5 0.1 reduce
  1.6 0.7 sub.30
  2.2 0.1 select_reduce_fusion
  2.3 0.6 maximum_subtract_fusion.low_ref
  2.9 1.4 broadcast_in_dim.20.gain_ref
  4.3 1.0 fusion
  5.3 1.0 pad_maximum_fusion
  6.3 88.0 %gather_and_project.1 = (bf16[512,5376]{1,0:T(8,128)(2,1)}, bf16[512,512]{1,0:T(8,128)(2,1)}, f32[512,256]{1,0:T(8,128)}, bf16[3,512,512]{2,1,0:T(8,128)(2,1)}) custom-call(bf16[128,5376]{1,0:T(8,128)(2,1)} %tokens_ref.1, f32[1,5376]{1,0:T(1,128)} %broadcast_in_dim.20.gain_ref, bf16[512,512]{1,0:T(8,128)(2,1)} %raw_hbm.3, f32[1,128]{1,0:T(1,128)} %bitcast.7, ...), custom_call_target="tpu_custom_call" | custom-call | flops 3000000000 | bytes 150000000 | tf_op jit(solution)/shard_map/gather_and_project/pallas_call | solution.py:397
  94.3 0.0 copy-start
  94.3 37.9 %attend_back.1 = (bf16[512,512]{1,0:T(8,128)(2,1)}, bf16[512,512]{1,0:T(8,128)(2,1)}) custom-call(bf16[512,512]{1,0:T(8,128)(2,1)} %get-tuple-element.14.query_ref, bf16[1536,512]{1,0:T(8,128)(2,1)} %bitcast.11, bf16[512,512]{1,0:T(8,128)(2,1)} %out_grad_hbm.1, s32[2,1,256]{2,1,0:T(1,128)} %maximum_subtract_fusion.low_ref, bf16[512,512]{1,0:T(8,128)(2,1)} %raw_hbm.3, ...), custom_call_target="tpu_custom_call" | custom-call | flops 8000000000 | bytes 100000000 | tf_op jit(solution)/shard_map/attend_back/pallas_call | solution.py:619
  132.3 0.0 copy-done
  132.3 0.0 copy-start.1
  132.3 1.0 copy-done.1
  133.3 82.3 %finish.1 = (f32[84,256]{1,0:T(8,128)S(1)}, f32[84,256]{1,0:T(8,128)S(1)}, bf16[128,5376]{1,0:T(8,128)(2,1)S(1)}) custom-call(bf16[512,5376]{1,0:T(8,128)(2,1)} %get-tuple-element.13.gathered_ref, bf16[512,512]{1,0:T(8,128)(2,1)S(1)} %copy-done.1, bf16[5376,256]{1,0:T(8,128)(2,1)} %w_key_ref.3, bf16[5376,256]{1,0:T(8,128)(2,1)} %w_value_ref.3, ...), custom_call_target="tpu_custom_call" | custom-call | flops 6000000000 | bytes 150000000 | tf_op jit(solution)/shard_map/finish/pallas_call | solution.py:945
  215.6 0.0 copy-start.2
  215.7 1.1 copy.20
  216.7 0.3 copy-done.2
  217.0 0.8 copy.21
  217.8 0.6 copy.22
  218.4 0.6 copy.23
  (3 shorter events, 0.0 us)
Async XLA Ops:
  94.3 38.0 %copy-start = (f32[1,5376]{1,0:T(1,128)S(1)}, f32[1,5376]{1,0:T(1,128)}, u32[]{:S(2)}) copy-start(f32[1,5376]{1,0:T(1,128)} %broadcast_in_dim.20.gain_ref) | copy-start | bytes 64516
  132.3 1.0 copy-start.1
  215.6 1.4 copy-start.2

commit v5 on v4

--- a/solution.py
+++ b/solution.py
@@ -25,12 +25,17 @@
 
 def angle_tables(positions, head_size):
     half_size = head_size // 2
-    powers = jnp.arange(half_size, dtype=jnp.float32) * (2.0 / head_size)
+    lane = jnp.arange(head_size, dtype=jnp.int32)
+    powers = (lane % half_size).astype(jnp.float32) * (2.0 / head_size)
     frequency = ROPE_BASE ** (-powers)
     angles = positions.astype(jnp.float32)[:, None] * frequency[None, :]
-    cosine = jnp.cos(angles)
-    sine = jnp.sin(angles)
-    return jnp.concatenate([cosine, cosine], axis=1), jnp.concatenate([-sine, sine], axis=1)
+    sign = jnp.where(lane < half_size, -1.0, 1.0)
+    return jnp.cos(angles), jnp.sin(angles) * sign[None, :]
+
+
+def one_row(blocks_ref, row_ref):
+    for index in range(blocks_ref.shape[0]):
+        row_ref[:, index * 128 : (index + 1) * 128] = blocks_ref[index : index + 1, :]
 
 
 def contract_last(left, right):
@@ -117,9 +122,9 @@
 
 
 def gather_kernel(
-    tokens_hbm, gain_ref, raw_hbm, q_gain_ref, k_gain_ref, cos_ref, sin_ref, w_key_ref, w_value_ref,
+    tokens_hbm, gain_blocks, raw_hbm, q_gain_ref, k_gain_ref, cos_ref, sin_ref, w_key_ref, w_value_ref,
     gathered_ref, query_ref, raw_key_ref, window_ref,
-    held, relay_up, relay_down, weights, window, tokens_ref, raw_ref, passing,
+    held, relay_up, relay_down, weights, window, tokens_ref, raw_ref, passing, gain_ref,
     weight_sem, out_sem, window_sem, relay_send, relay_recv, cross_send, cross_recv,
     pair_send, pair_recv, chunk_send, chunk_recv, halo_send, halo_recv, middle_send, middle_recv,
 ):
@@ -192,6 +197,7 @@
         ).astype(jnp.bfloat16)
         return carry
 
+    one_row(gain_blocks, gain_ref)
     load_tokens.wait()
     lax.fori_loop(0, rows // 16, norm_rows, 0)
     pl.semaphore_wait(barrier, 9)
@@ -413,6 +419,7 @@
             pltpu.VMEM((rows, depth), bf),
             pltpu.VMEM(raw_queries.shape, bf),
             pltpu.VMEM((shard, 2 * cols), bf),
+            pltpu.VMEM((1, depth), jnp.float32),
             dma((4,)),
             dma((4,)),
             dma((1,)),
@@ -436,7 +443,7 @@
             flops=3_000_000_000, bytes_accessed=150_000_000, transcendentals=0
         ),
         name="gather_and_project",
-    )(tokens, in_gain[None, :], raw_queries, q_gain[None, :], k_gain[None, :], cosine, sine, w_key, w_value)
+    )(tokens, in_gain.reshape(depth // 128, 128), raw_queries, q_gain[None, :], k_gain[None, :], cosine, sine, w_key, w_value)
 
 
 def unturn(values, cosine, sine):
@@ -454,7 +461,7 @@
     query_ref, window_ref, out_grad_hbm, low_ref, raw_hbm, raw_key_ref, cos_ref, sin_ref, q_gain_ref, k_gain_ref,
     grad_query_ref, grad_kv_ref,
     exps, along, totals, query_total, parts, returned, out_grad_ref, raw_ref, passing,
-    send_sem, recv_sem, middle_send, middle_recv, load_sem,
+    send_sem, recv_sem, middle_send, middle_recv, load_sem, chain_send, chain_recv, sum_send, sum_recv,
 ):
     shard = query_ref.shape[0]
     head_size = q_gain_ref.shape[1]
@@ -506,6 +513,30 @@
             send_sem=middle_send.at[head],
             recv_sem=middle_recv.at[head],
             device_id=middle_to,
+            device_id_type=MESH_IDS,
+        )
+
+    last = kv_heads - 1
+
+    def chain(piece):
+        at = pl.ds(piece * tile, tile)
+        return pltpu.make_async_remote_copy(
+            src_ref=parts.at[0, last, at],
+            dst_ref=passing.at[last, at],
+            send_sem=chain_send.at[piece],
+            recv_sem=chain_recv.at[piece],
+            device_id=earlier,
+            device_id_type=MESH_IDS,
+        )
+
+    def summed(piece):
+        at = pl.ds(piece * tile, tile)
+        return pltpu.make_async_remote_copy(
+            src_ref=parts.at[1, last, at],
+            dst_ref=returned.at[1, last, at],
+            send_sem=sum_send.at[piece],
+            recv_sem=sum_recv.at[piece],
+            device_id=earlier,
             device_id_type=MESH_IDS,
         )
 
@@ -573,27 +604,48 @@
             return carry
 
         lax.fori_loop(0, 2, half, 0)
-        for window in range(2):
+        for window in range(2 if head < last else 1):
             rows = slice(window * shard, (window + 1) * shard)
             parts[window, head, :, :head_size] = totals[rows, key_lanes].astype(jnp.bfloat16)
             parts[window, head, :, head_size:] = totals[rows, value_lanes].astype(jnp.bfloat16)
         if head == 0:
             pl.semaphore_wait(barrier, 6)
-        middle(head).start()
-        back(1, head).start()
-
-    for head in range(kv_heads):
+        if head < last:
+            middle(head).start()
+            back(1, head).start()
+        else:
+            chain(0).start()
+            chain(1).start()
+
+    for head in range(last):
         middle(head).wait_recv()
         back(0, head).start()
+    for piece in range(2):
+        chain(piece).wait_recv()
+        here = slice(piece * tile, (piece + 1) * tile)
+        rows = slice(shard + piece * tile, shard + (piece + 1) * tile)
+        lanes = slice(last * head_size, (last + 1) * head_size)
+        parts[1, last, here, :head_size] = (
+            totals[rows, lanes] + passing[last, here, :head_size].astype(jnp.float32)
+        ).astype(jnp.bfloat16)
+        lanes = slice((kv_heads + last) * head_size, (kv_heads + last + 1) * head_size)
+        parts[1, last, here, head_size:] = (
+            totals[rows, lanes] + passing[last, here, head_size:].astype(jnp.float32)
+        ).astype(jnp.bfloat16)
+        summed(piece).start()
     own = slice(reach, reach + shard)
     for head in range(kv_heads):
         key_lanes = slice(head * head_size, (head + 1) * head_size)
         value_lanes = slice((kv_heads + head) * head_size, (kv_heads + head + 1) * head_size)
-        for window in range(2):
-            back(window, head).wait_recv()
+        if head < last:
+            for window in range(2):
+                back(window, head).wait_recv()
+        else:
+            summed(0).wait_recv()
+            summed(1).wait_recv()
         key_grad = totals[own, key_lanes]
         value_grad = totals[own, value_lanes]
-        for window in (1, 0):
+        for window in (1, 0) if head < last else (1,):
             key_grad = key_grad + returned[window, head, :, :head_size].astype(jnp.float32)
             value_grad = value_grad + returned[window, head, :, head_size:].astype(jnp.float32)
         grad_kv_ref[:, value_lanes] = value_grad.astype(jnp.bfloat16)
@@ -601,10 +653,13 @@
         grad_kv_ref[:, key_lanes] = norm_back(key_grad, raw_key_ref[:, key_lanes], k_gain_ref[...]).astype(
             jnp.bfloat16
         )
-    for head in range(kv_heads):
+    for head in range(last):
         middle(head).wait_send()
         for window in range(2):
             back(window, head).wait_send()
+    for piece in range(2):
+        chain(piece).wait_send()
+        summed(piece).wait_send()
 
 
 def attend_back(query_rot, window, out_grad, low, raw_queries, raw_keys, cosine, sine, q_gain, k_gain):
@@ -639,6 +694,10 @@
             pltpu.SemaphoreType.DMA((kv_heads,)),
             pltpu.SemaphoreType.DMA((kv_heads,)),
             pltpu.SemaphoreType.DMA((2,)),
+            pltpu.SemaphoreType.DMA((2,)),
+            pltpu.SemaphoreType.DMA((2,)),
+            pltpu.SemaphoreType.DMA((2,)),
+            pltpu.SemaphoreType.DMA((2,)),
         ],
         compiler_params=pltpu.CompilerParams(
             collective_id=3, has_side_effects=True, vmem_limit_bytes=60 * 1024 * 1024
@@ -654,16 +713,17 @@
 
 
 def finish_kernel(
-    gathered_ref, grad_ref, w_key_ref, w_value_ref, tokens_ref, gain_ref,
+    gathered_ref, grad_ref, w_key_ref, w_value_ref, tokens_ref, gain_blocks,
     key_out, value_out, grad_x_ref,
-    held, weights, tokens, total_own, corner_out, corner_in, beside_out, beside_in, cross_out, cross_in,
+    held, weights, tokens, gain_ref, total_own, corner_out, corner_in, beside_out, beside_in, cross_out, cross_in,
     relay_up, relay_down,
     key_term, value_term, key_send, order, value_total, key_next, value_next, last_send, last_recv,
     *rest,
 ):
     bufs_a, bufs_b, bufs_c, bufs_d = rest[0:6], rest[6:12], rest[12:18], rest[18:24]
     sems = rest[24:34]
-    load_sem, weight_sem, pair_send, pair_recv, relay_send, relay_recv, cross_send, cross_recv = rest[34:]
+    load_sem, weight_sem, pair_send, pair_recv, relay_send, relay_recv, cross_send, cross_recv = rest[34:42]
+    corner_send, corner_recv = rest[42:]
     depth = gain_ref.shape[1]
     block = tokens_ref.shape[0]
     rows = key_out.shape[0]
@@ -748,25 +808,25 @@
 
     part(corner, store_corner, first=True)
     pl.semaphore_wait(barrier, 10)
-    send_corner = remote(corner_out, corner_in, pair_send.at[0], pair_recv.at[0], partner)
-    send_corner.start()
+
+    def rows_at(side, step):
+        return pl.ds(side * half + step * piece, piece)
+
+    pieces = [(side, step) for step in range(4) for side in (0, 1)]
+    send_corner = {
+        (side, step): remote(
+            corner_out.at[rows_at(side, step)], corner_in.at[rows_at(side, step)],
+            corner_send.at[side, step], corner_recv.at[side, step], partner,
+        )
+        for side, step in pieces
+    }
+    for one in pieces:
+        send_corner[one].start()
 
     def store_total(at, value):
         total_own[:, at] = value
 
     part(across, store_total)
-    send_corner.wait_recv()
-
-    def join(step, carry):
-        at = pl.ds(pl.multiple_of(step * 16, 16), 16)
-        cross_out[at, :] = (total_own[at, :] + corner_in[at, :].astype(jnp.float32)).astype(jnp.bfloat16)
-        return carry
-
-    lax.fori_loop(0, block // 16, join, 0)
-
-    def rows_at(side, step):
-        return pl.ds(side * half + step * piece, piece)
-
     def small(step):
         return pl.ds(step * piece, piece)
 
@@ -784,9 +844,11 @@
         ]
         for step in range(4)
     ]
-    for pair in first:
-        for one in pair:
-            one.start()
+    for side, step in pieces:
+        send_corner[side, step].wait_recv()
+        at = rows_at(side, step)
+        cross_out[at, :] = (total_own[at, :] + corner_in[at, :].astype(jnp.float32)).astype(jnp.bfloat16)
+        first[step][side].start()
 
     def relay(step):
         for side in (0, 1):
@@ -886,6 +948,7 @@
         one.start()
         copies.append(one)
 
+    one_row(gain_blocks, gain_ref)
     load_tokens.wait()
     send_beside.wait_recv()
     for step in range(4):
@@ -910,7 +973,8 @@
         one.wait_send()
     for drain in (drain_a, drain_b, drain_c, drain_d):
         drain()
-    send_corner.wait_send()
+    for one in pieces:
+        send_corner[one].wait_send()
     send_beside.wait_send()
     for pair in first + second:
         for one in pair:
@@ -955,6 +1019,7 @@
             pltpu.VMEM((shard, depth), bf),
             pltpu.VMEM((depth, 2 * cols), bf),
             pltpu.VMEM((block, depth), bf),
+            pltpu.VMEM((1, depth), jnp.float32),
             pltpu.VMEM((block, depth), jnp.float32),
         ]
         + [pltpu.VMEM((block, depth), bf)] * 6
@@ -977,7 +1042,7 @@
         + [dma((6,))] * 8
         + [dma((3,))] * 2
         + [dma((2,)), dma((2, slabs)), dma((2,)), dma((2,))]
-        + [dma((2, 4))] * 4,
+        + [dma((2, 4))] * 6,
         compiler_params=pltpu.CompilerParams(
             collective_id=1, has_side_effects=True, vmem_limit_bytes=51 * 1024 * 1024
         ),
@@ -985,7 +1050,7 @@
             flops=6_000_000_000, bytes_accessed=150_000_000, transcendentals=0
         ),
         name="finish",
-    )(gathered, grad_kv, w_key, w_value, tokens, in_gain[None, :])
+    )(gathered, grad_kv, w_key, w_value, tokens, in_gain.reshape(depth // 128, 128))
 
 
 def shards(tokens, in_gain, raw_queries, w_key, w_value, q_gain, k_gain, doc_lengths, out_grad):

time: 223 us -> 215 us (0.964); the launches traced: 219 us -> 215 us
  no operation moved by 1% of the time
where the time goes in v5:
time: 215 us
  Pallas kernels  206 us (96%)
  local copies, waits for them, and re-layouts  5.21 us (2%)
  other arithmetic  3.33 us (2%)
    pallas_call x1, Pallas kernels, gather_and_project(): pl.pallas_call(gather_kernel, out_shape=[jax.ShapeDtypeStruct((shard, dep...  88 us
    pallas_call x1, Pallas kernels, finish(): pl.pallas_call(finish_kernel, out_shape=[jax.ShapeDtypeStruct((rows, cols...  81.5 us
    pallas_call x1, Pallas kernels, attend_back(): pl.pallas_call(attend_kernel, out_shape=[jax.ShapeDtypeStruct(query_rot.s...  36.5 us
    unnamed x10, local copies, waits for them, and re-layouts  4.47 us

profile of v5, /device:TPU:61, one launch (start us, length us, event | category | flops | bytes accessed | tf_op | source)
XLA Modules:
  0.0 215.2 jit_solution(10111782663379440875)
XLA Ops:
  0.7 0.7 copy.15
  1.4 0.1 reduce-window.9
  1.5 0.1 reduce
  1.6 0.7 sub.30
  2.2 0.1 select_reduce_fusion
  2.3 0.6 maximum_subtract_fusion.low_ref
  2.9 1.8 fusion
  4.7 88.0 %gather_and_project.1 = (bf16[512,5376]{1,0:T(8,128)(2,1)}, bf16[512,512]{1,0:T(8,128)(2,1)}, f32[512,256]{1,0:T(8,128)}, bf16[3,512,512]{2,1,0:T(8,128)(2,1)}) custom-call(bf16[128,5376]{1,0:T(8,128)(2,1)} %tokens_ref.1, f32[42,128]{1,0:T(8,128)} %bitcast.6, bf16[512,512]{1,0:T(8,128)(2,1)} %raw_hbm.3, f32[1,128]{1,0:T(1,128)} %bitcast.10, ...), custom_call_target="tpu_custom_call" | custom-call | flops 3000000000 | bytes 150000000 | tf_op jit(solution)/shard_map/gather_and_project/pallas_call | solution.py:403
  92.7 0.0 copy-start
  92.7 36.5 %attend_back.1 = (bf16[512,512]{1,0:T(8,128)(2,1)}, bf16[512,512]{1,0:T(8,128)(2,1)}) custom-call(bf16[512,512]{1,0:T(8,128)(2,1)} %get-tuple-element.14.query_ref, bf16[1536,512]{1,0:T(8,128)(2,1)} %bitcast.14, bf16[512,512]{1,0:T(8,128)(2,1)} %out_grad_hbm.1, s32[2,1,256]{2,1,0:T(1,128)} %maximum_subtract_fusion.low_ref, bf16[512,512]{1,0:T(8,128)(2,1)} %raw_hbm.3, ...), custom_call_target="tpu_custom_call" | custom-call | flops 8000000000 | bytes 100000000 | tf_op jit(solution)/shard_map/attend_back/pallas_call | solution.py:674
  129.3 0.0 copy-done
  129.3 0.0 copy-start.1
  129.3 1.0 copy-done.1
  130.3 81.5 %finish.1 = (f32[84,256]{1,0:T(8,128)S(1)}, f32[84,256]{1,0:T(8,128)S(1)}, bf16[128,5376]{1,0:T(8,128)(2,1)S(1)}) custom-call(bf16[512,5376]{1,0:T(8,128)(2,1)} %get-tuple-element.13.gathered_ref, bf16[512,512]{1,0:T(8,128)(2,1)S(1)} %copy-done.1, bf16[5376,256]{1,0:T(8,128)(2,1)} %w_key_ref.3, bf16[5376,256]{1,0:T(8,128)(2,1)} %w_value_ref.3, ...), custom_call_target="tpu_custom_call" | custom-call | flops 6000000000 | bytes 150000000 | tf_op jit(solution)/shard_map/finish/pallas_call | solution.py:1009
  211.8 0.0 copy-start.2
  211.8 1.1 copy.20
  212.9 0.3 copy-done.2
  213.2 0.8 copy.21
  214.0 0.6 copy.22
  214.6 0.6 copy.23
  (3 shorter events, 0.0 us)
Async XLA Ops:
  92.7 36.5 %copy-start = (f32[5376]{0:T(1024)S(1)}, f32[5376]{0:T(1024)}, u32[]{:S(2)}) copy-start(f32[5376]{0:T(1024)} %param.10) | copy-start | bytes 64516
  129.3 1.0 copy-start.1
  211.8 1.4 copy-start.2

commit v6 on v5

--- a/solution.py
+++ b/solution.py
@@ -156,6 +156,8 @@
 
     left, right = lax.rem(x + WIDE - 1, WIDE), lax.rem(x + 1, WIDE)
     row_left, row_right = in_row(place, left), in_row(place, right)
+    direct_to = (lax.rem(place + 2, count), member)
+    direct_from = (lax.rem(place + count - 2, count), member)
     second_to = (lax.rem(place // WIDE * WIDE + right + 2, count), member)
     second_from = in_row(lax.rem(place + count - 2, count), lax.rem(x + 2 * WIDE - 3, WIDE))
 
@@ -180,7 +182,7 @@
     for one in loads:
         one.start()
     barrier = pltpu.get_barrier_semaphore()
-    for other in [z_up, z_down, partner, later, earlier, second_to, second_from, row_left, row_right]:
+    for other in [z_up, z_down, partner, later, earlier, direct_to, direct_from, second_to, second_from, row_left, row_right]:
         pl.semaphore_signal(barrier, inc=1, device_id=other, device_id_type=MESH_IDS)
 
     own = pl.multiple_of(member * rows, rows)
@@ -200,7 +202,7 @@
     one_row(gain_blocks, gain_ref)
     load_tokens.wait()
     lax.fori_loop(0, rows // 16, norm_rows, 0)
-    pl.semaphore_wait(barrier, 9)
+    pl.semaphore_wait(barrier, 11)
 
     to_partner = remote(
         held.at[pl.ds(own, rows)], held.at[pl.ds(own, rows)], pair_send.at[0], pair_recv.at[0], partner
@@ -259,6 +261,12 @@
         at = pl.ds(begin, size)
         return remote(
             window.at[2, at], passing.at[at], middle_send.at[index], middle_recv.at[index], row_left
+        )
+
+    def direct(index, begin, size):
+        at = pl.ds(begin, size)
+        return remote(
+            window.at[2, at], window.at[0, at], halo_send.at[1, index], halo_recv.at[1, index], direct_to
         )
 
     def hand_on(index, begin, size):
@@ -347,12 +355,22 @@
         project(groups(step))
         for index, (begin, size) in enumerate(groups(step)):
             halo(1, 2 + step * 4 + index, begin, size).start()
-            middle(2 + step * 4 + index, begin, size).start()
+
+        @pl.when(step < 3)
+        def over_middle():
+            for index, (begin, size) in enumerate(groups(step)):
+                middle(2 + step * 4 + index, begin, size).start()
+
+        @pl.when(step == 3)
+        def at_last():
+            for index, (begin, size) in enumerate(groups(step)):
+                direct(2 + step * 4 + index, begin, size).start()
+
         return carry
 
     lax.fori_loop(0, 4, arrive, 0)
-    for index, (begin, size) in enumerate(groups(3)):
-        hand_on(14 + index, begin, size)
+    out_mine = pltpu.make_async_copy(window.at[2], window_ref.at[2], window_sem.at[0])
+    out_mine.start()
     out_across = pltpu.make_async_copy(
         held.at[pl.ds(across, rows)], gathered_ref.at[pl.ds(across, rows)], out_sem.at[2]
     )
@@ -362,23 +380,33 @@
     out_across.start()
     out_corner.start()
 
-    def each_halo(kinds, act):
-        for kind in kinds:
-            act(kind(0, own, rows))
-            act(kind(1, beside, rows))
-
-            def inner(step, carry):
-                for index, (begin, size) in enumerate(groups(step)):
-                    act(kind(2 + step * 4 + index, begin, size))
-                return carry
-
-            lax.fori_loop(0, 4, inner, 0)
-
-    halos = [functools.partial(halo, 1), functools.partial(halo, 2)]
-    each_halo(halos, lambda copy: copy.wait_recv())
-    out_window = pltpu.make_async_copy(window, window_ref, window_sem.at[0])
+    def each_halo(kind, steps, act):
+        act(kind(0, own, rows))
+        act(kind(1, beside, rows))
+
+        def inner(step, carry):
+            for index, (begin, size) in enumerate(groups(step)):
+                act(kind(2 + step * 4 + index, begin, size))
+            return carry
+
+        lax.fori_loop(0, steps, inner, 0)
+
+    def last_direct(act):
+        for index, (begin, size) in enumerate(groups(3)):
+            act(direct(14 + index, begin, size))
+
+    one_on, two_on = functools.partial(halo, 1), functools.partial(halo, 2)
+    each_halo(one_on, 4, lambda copy: copy.wait_recv())
+    each_halo(two_on, 3, lambda copy: copy.wait_recv())
+    last_direct(lambda copy: copy.wait_recv())
+    out_window = pltpu.make_async_copy(
+        window.at[pl.ds(0, 2)], window_ref.at[pl.ds(0, 2)], window_sem.at[1]
+    )
     out_window.start()
-    each_halo(halos + [middle], lambda copy: copy.wait_send())
+    each_halo(one_on, 4, lambda copy: copy.wait_send())
+    each_halo(two_on, 3, lambda copy: copy.wait_send())
+    each_halo(middle, 3, lambda copy: copy.wait_send())
+    last_direct(lambda copy: copy.wait_send())
     to_partner.wait_send()
     for step in range(4):
         first_up(step).wait_send()
@@ -387,7 +415,7 @@
         second_down(step).wait_send()
         pass_on(0, step).wait_send()
         pass_on(1, step).wait_send()
-    for one in (out_own, out_beside, out_across, out_corner, out_window):
+    for one in (out_own, out_beside, out_across, out_corner, out_mine, out_window):
         one.wait()
 
 
@@ -422,7 +450,7 @@
             pltpu.VMEM((1, depth), jnp.float32),
             dma((4,)),
             dma((4,)),
-            dma((1,)),
+            dma((2,)),
             dma((2, 4)),
             dma((2, 4)),
             dma((2, 4)),
@@ -561,14 +589,18 @@
             high = lax.broadcasted_iota(jnp.int32, (1, tile), 1) + (reach + begin)
             high = jnp.concatenate([high] * group_size, axis=1)
 
-            def scores(index, stats):
+            inner_key = lax.broadcasted_iota(jnp.int32, (tile, width), 0)
+
+            def scores(index, stats, diagonal=False):
                 total, delta = stats
                 first = pl.multiple_of(begin + index * tile, tile)
                 key_rows = pl.ds(first, tile)
                 score = across(window_ref[key_rows, key_lanes], queries)
                 partial = across(window_ref[key_rows, value_lanes], grads)
-                key = lax.broadcasted_iota(jnp.int32, (tile, width), 0) + first
-                value = jnp.where((key >= low) & (key <= high), jnp.exp(score), 0.0)
+                allowed = inner_key >= low - first
+                if diagonal:
+                    allowed = allowed & (inner_key <= high - first)
+                value = jnp.where(allowed, jnp.exp(score), 0.0)
                 at = pl.ds(pl.multiple_of(index * tile, tile), tile)
                 exps[at, :] = value
                 along[at, :] = partial
@@ -577,7 +609,8 @@
                 return total, delta
 
             nothing = jnp.zeros((1, width), jnp.float32)
-            total, delta = lax.fori_loop(0, reach // tile + 1, scores, (nothing, nothing))
+            stats = lax.fori_loop(0, reach // tile, scores, (nothing, nothing))
+            total, delta = scores(reach // tile, stats, diagonal=True)
             inverse = 1.0 / total
             delta = delta * inverse
             query_total[...] = jnp.zeros_like(query_total)

time: 215 us -> 214 us (level)
  no operation moved by 1% of the time
where the time goes in v6:
time: 214 us
  Pallas kernels  205 us (96%)
  local copies, waits for them, and re-layouts  5.21 us (2%)
  other arithmetic  3.33 us (2%)
    pallas_call x1, Pallas kernels, gather_and_project(): pl.pallas_call(gather_kernel, out_shape=[jax.ShapeDtypeStruct((shard, dep...  87.2 us
    pallas_call x1, Pallas kernels, finish(): pl.pallas_call(finish_kernel, out_shape=[jax.ShapeDtypeStruct((rows, cols...  82.8 us
    pallas_call x1, Pallas kernels, attend_back(): pl.pallas_call(attend_kernel, out_shape=[jax.ShapeDtypeStruct(query_rot.s...  34.9 us
    unnamed x10, local copies, waits for them, and re-layouts  4.47 us

profile of v6, /device:TPU:61, one launch (start us, length us, event | category | flops | bytes accessed | tf_op | source)
XLA Modules:
  0.0 214.1 jit_solution(8246930677109045373)
XLA Ops:
  0.7 0.7 copy.15
  1.4 0.1 reduce-window.9
  1.5 0.1 reduce
  1.6 0.7 sub.30
  2.2 0.1 select_reduce_fusion
  2.3 0.6 maximum_subtract_fusion.low_ref
  2.9 1.8 fusion
  4.7 87.2 %gather_and_project.1 = (bf16[512,5376]{1,0:T(8,128)(2,1)}, bf16[512,512]{1,0:T(8,128)(2,1)}, f32[512,256]{1,0:T(8,128)}, bf16[3,512,512]{2,1,0:T(8,128)(2,1)}) custom-call(bf16[128,5376]{1,0:T(8,128)(2,1)} %tokens_ref.1, f32[42,128]{1,0:T(8,128)} %bitcast.6, bf16[512,512]{1,0:T(8,128)(2,1)} %raw_hbm.3, f32[1,128]{1,0:T(1,128)} %bitcast.10, ...), custom_call_target="tpu_custom_call" | custom-call | flops 3000000000 | bytes 150000000 | tf_op jit(solution)/shard_map/gather_and_project/pallas_call | solution.py:431
  91.9 0.0 copy-start
  92.0 34.9 %attend_back.1 = (bf16[512,512]{1,0:T(8,128)(2,1)}, bf16[512,512]{1,0:T(8,128)(2,1)}) custom-call(bf16[512,512]{1,0:T(8,128)(2,1)} %get-tuple-element.14.query_ref, bf16[1536,512]{1,0:T(8,128)(2,1)} %bitcast.14, bf16[512,512]{1,0:T(8,128)(2,1)} %out_grad_hbm.1, s32[2,1,256]{2,1,0:T(1,128)} %maximum_subtract_fusion.low_ref, bf16[512,512]{1,0:T(8,128)(2,1)} %raw_hbm.3, ...), custom_call_target="tpu_custom_call" | custom-call | flops 8000000000 | bytes 100000000 | tf_op jit(solution)/shard_map/attend_back/pallas_call | solution.py:707
  126.8 0.0 copy-done
  126.8 0.0 copy-start.1
  126.8 1.0 copy-done.1
  127.9 82.8 %finish.1 = (f32[84,256]{1,0:T(8,128)S(1)}, f32[84,256]{1,0:T(8,128)S(1)}, bf16[128,5376]{1,0:T(8,128)(2,1)S(1)}) custom-call(bf16[512,5376]{1,0:T(8,128)(2,1)} %get-tuple-element.13.gathered_ref, bf16[512,512]{1,0:T(8,128)(2,1)S(1)} %copy-done.1, bf16[5376,256]{1,0:T(8,128)(2,1)} %w_key_ref.3, bf16[5376,256]{1,0:T(8,128)(2,1)} %w_value_ref.3, ...), custom_call_target="tpu_custom_call" | custom-call | flops 6000000000 | bytes 150000000 | tf_op jit(solution)/shard_map/finish/pallas_call | solution.py:1042
  210.7 0.0 copy-start.2
  210.7 1.1 copy.20
  211.8 0.3 copy-done.2
  212.0 0.8 copy.21
  212.8 0.6 copy.22
  213.5 0.6 copy.23
  (3 shorter events, 0.0 us)
Async XLA Ops:
  91.9 34.9 %copy-start = (f32[5376]{0:T(1024)S(1)}, f32[5376]{0:T(1024)}, u32[]{:S(2)}) copy-start(f32[5376]{0:T(1024)} %param.10) | copy-start | bytes 64516
  126.8 1.0 copy-start.1
  210.7 1.4 copy-start.2

commit v7 on v6

--- a/solution.py
+++ b/solution.py
@@ -465,7 +465,7 @@
             dma((18,)),
         ],
         compiler_params=pltpu.CompilerParams(
-            collective_id=2, has_side_effects=True, vmem_limit_bytes=60 * 1024 * 1024
+            collective_id=2, has_side_effects=True, vmem_limit_bytes=57 * 1024 * 1024
         ),
         cost_estimate=pl.CostEstimate(
             flops=3_000_000_000, bytes_accessed=150_000_000, transcendentals=0
@@ -733,7 +733,7 @@
             pltpu.SemaphoreType.DMA((2,)),
         ],
         compiler_params=pltpu.CompilerParams(
-            collective_id=3, has_side_effects=True, vmem_limit_bytes=60 * 1024 * 1024
+            collective_id=3, has_side_effects=True, vmem_limit_bytes=52 * 1024 * 1024
         ),
         cost_estimate=pl.CostEstimate(
             flops=8_000_000_000, bytes_accessed=100_000_000, transcendentals=3_000_000

time: 214 us -> 212 us (level)
    unnamed x10 -> x14, local copies, waits for them, and re-layouts: 4.47 us -> 3.17 us
where the time goes in v7:
time: 212 us; the launch traced here: 211 us
  Pallas kernels  204 us (96%)
  local copies, waits for them, and re-layouts  3.91 us (2%)
  other arithmetic  2.78 us (1%)
    pallas_call x1, Pallas kernels, gather_and_project(): pl.pallas_call(gather_kernel, out_shape=[jax.ShapeDtypeStruct((shard, dep...  87.4 us
    pallas_call x1, Pallas kernels, finish(): pl.pallas_call(finish_kernel, out_shape=[jax.ShapeDtypeStruct((rows, cols...  83 us
    pallas_call x1, Pallas kernels, attend_back(): pl.pallas_call(attend_kernel, out_shape=[jax.ShapeDtypeStruct(query_rot.s...  33.6 us

profile of v7, /device:TPU:61, one launch (start us, length us, event | category | flops | bytes accessed | tf_op | source)
XLA Modules:
  0.0 211.5 jit_solution(2237578837785705370)
XLA Ops:
  0.7 0.7 copy.15
  1.4 0.1 reduce-window.9
  1.5 0.1 reduce
  1.6 0.7 sub.30
  2.2 0.1 select_reduce_fusion
  2.4 1.8 fusion
  4.2 0.0 copy-start
  4.2 0.0 copy-start.1
  4.2 0.0 copy-start.3
  4.2 0.0 copy-start.4
  4.2 87.4 %gather_and_project.1 = (bf16[512,5376]{1,0:T(8,128)(2,1)}, bf16[512,512]{1,0:T(8,128)(2,1)}, f32[512,256]{1,0:T(8,128)}, bf16[3,512,512]{2,1,0:T(8,128)(2,1)}) custom-call(bf16[128,5376]{1,0:T(8,128)(2,1)} %tokens_ref.1, f32[42,128]{1,0:T(8,128)} %bitcast.6, bf16[512,512]{1,0:T(8,128)(2,1)} %raw_hbm.3, f32[1,128]{1,0:T(1,128)} %bitcast.8, ...), custom_call_target="tpu_custom_call" | custom-call | flops 3000000000 | bytes 150000000 | tf_op jit(solution)/shard_map/gather_and_project/pallas_call | solution.py:431
  91.6 0.0 copy-done
  91.6 0.0 copy-done.1
  91.6 0.0 copy-done.3
  91.6 0.0 copy-done.4
  91.7 0.0 copy-start.2
  91.7 33.6 %attend_back.1 = (bf16[512,512]{1,0:T(8,128)(2,1)S(1)}, bf16[512,512]{1,0:T(8,128)(2,1)S(1)}) custom-call(bf16[512,512]{1,0:T(8,128)(2,1)} %get-tuple-element.14.query_ref, bf16[1536,512]{1,0:T(8,128)(2,1)} %bitcast.14, bf16[512,512]{1,0:T(8,128)(2,1)} %out_grad_hbm.1, s32[2,1,256]{2,1,0:T(1,128)S(1)} %maximum_subtract_fusion.low_ref, ...), custom_call_target="tpu_custom_call" | custom-call | flops 8000000000 | bytes 100000000 | tf_op jit(solution)/shard_map/attend_back/pallas_call | solution.py:707
  125.3 0.0 copy-done.2
  125.3 83.0 %finish.1 = (f32[84,256]{1,0:T(8,128)S(1)}, f32[84,256]{1,0:T(8,128)S(1)}, bf16[128,5376]{1,0:T(8,128)(2,1)S(1)}) custom-call(bf16[512,5376]{1,0:T(8,128)(2,1)} %get-tuple-element.13.gathered_ref, bf16[512,512]{1,0:T(8,128)(2,1)S(1)} %get-tuple-element.17.grad_ref, bf16[5376,256]{1,0:T(8,128)(2,1)} %w_key_ref.3, bf16[5376,256]{1,0:T(8,128)(2,1)} %w_value_ref.3, ...), custom_call_target="tpu_custom_call" | custom-call | flops 6000000000 | bytes 150000000 | tf_op jit(solution)/shard_map/finish/pallas_call | solution.py:1042
  208.3 1.1 copy.20
  209.4 0.8 copy.21
  210.2 0.6 copy.22
  210.8 0.6 copy.23
  (4 shorter events, 0.0 us)
Async XLA Ops:
  4.2 87.4 %copy-start = (f32[512,128]{1,0:T(8,128)S(1)}, f32[512,128]{1,0:T(8,128)}, u32[]{:S(2)}) copy-start(f32[512,128]{1,0:T(8,128)} %get-tuple-element.22.sin_ref) | copy-start | bytes 786436
  4.2 87.4 %copy-start.1 = (f32[512,128]{1,0:T(8,128)S(1)}, f32[512,128]{1,0:T(8,128)}, u32[]{:S(2)}) copy-start(f32[512,128]{1,0:T(8,128)} %get-tuple-element.23.cos_ref) | copy-start | bytes 786436
  4.2 87.4 %copy-start.3 = (f32[128]{0:T(128)S(1)}, f32[128]{0:T(128)}, u32[]{:S(2)}) copy-start(f32[128]{0:T(128)} %param.14) | copy-start | bytes 1540
  4.2 87.4 %copy-start.4 = (f32[128]{0:T(128)S(1)}, f32[128]{0:T(128)}, u32[]{:S(2)}) copy-start(f32[128]{0:T(128)} %param.15) | copy-start | bytes 1540
  91.7 33.6 %copy-start.2 = (f32[5376]{0:T(1024)S(1)}, f32[5376]{0:T(1024)}, u32[]{:S(2)}) copy-start(f32[5376]{0:T(1024)} %param.10) | copy-start | bytes 64516
